TPU v7x, 128 devices: a whole 4x4x4 slice. The times are simulated.
128 devices in a mesh: gx: 32 (over y, x, core), ba: 4 (over z).
Axes of the slice: x: 4, y: 4, z: 4, core: 2. Of those that a mesh axis runs over, the one named last changes fastest.
Arguments:
- phi_start: float32 [64, 16, 256, 256], P('gx', 'ba'), may hold values from -6 to 6
- coeff: float32 [64, 256, 256], P('gx'), may hold values from 1 to 3
- forward: float32 [2, 2, 64, 256, 256], P(None, None, None, 'gx'), may hold values from -6 to 6
- rates: float32 [16], P('ba'), may hold values from 0.02 to 0.2
- speeds: float32 [16], P('ba'), may hold values from 0.5 to 2
- shares: float32 [16], P('ba'), may hold values from 0.02 to 0.12
Outputs:
- phi_out: float32 [64, 16, 256, 256], P('gx', 'ba')
- grad: float32 [64, 12, 16], P('gx', None, 'ba')
All inputs are finite; a program needn't handle non-finite values.
Results may differ from a plain program's by a relative error of at most 0.00026.
Values sent between devices are 32-bit elements; how exact they have to be, the bound alone decides.
A program may use at most 128 MiB of HBM per device.

v0:
```python
import functools
import math

import jax
import jax.numpy as jnp
import numpy as np
from jax import lax
from jax.experimental import pallas as pl
from jax.experimental.pallas import tpu as pltpu
from jax.sharding import PartitionSpec as P

MESH = pl.DeviceIdType.MESH
N = 256
HALF = 128
GX = 32
BA = 4
ROWS = 8
BASE = 1.5 * 2.0 * math.pi / N


def quadrature():
    level = np.arange(6)
    polar = 0.2 + 0.15 * level
    cosine = np.concatenate([-polar, polar])
    azimuth = np.concatenate([level * (math.pi / 3.0) + math.pi / 6.0, level * (math.pi / 3.0)])
    sine = np.sqrt(1.0 - cosine * cosine)
    return cosine, sine * np.cos(azimuth), sine * np.sin(azimuth)


COS, SX, SY = quadrature()


def halves(table):
    table = jnp.asarray(table, jnp.float32)
    high = table.astype(jnp.bfloat16)
    return high, (table - high.astype(jnp.float32)).astype(jnp.bfloat16)


def np_halves(table):
    table = np.asarray(table, np.float32)
    high = table.astype(jnp.bfloat16)
    low = (table - high.astype(np.float32)).astype(jnp.bfloat16)
    return [jnp.asarray(high), jnp.asarray(low)]


def tables():
    index = np.arange(N)
    angle = (index[:, None] * index[None, :] % N) * (2.0 * np.pi / N)
    cos, sin = np.cos(angle) / 16.0, np.sin(angle) / 16.0
    rows = np.concatenate([cos[:, :HALF], -sin[:, :HALF]], axis=1)
    rows[:, HALF] = cos[:, HALF]
    back = np.concatenate([2.0 * cos[:HALF], -2.0 * sin[:HALF]], axis=0)
    back[0] = cos[0]
    back[HALF] = cos[HALF]
    return np_halves(rows), np_halves(back), np_halves(cos), np_halves(sin)


def split(value):
    high = value.astype(jnp.bfloat16)
    return high, (value - high.astype(jnp.float32)).astype(jnp.bfloat16)


def product(left, right):
    lh, ll = left
    rh, rl = right
    dot = functools.partial(jnp.dot, preferred_element_type=jnp.float32)
    return dot(lh, rh) + (dot(ll, rh) + dot(lh, rl))


def forward_kernel(phi, wh, wl, ch, cl, sh, sl, out, edge):
    edge[...] = jnp.zeros_like(edge)
    cos, sin = (ch[...], cl[...]), (sh[...], sl[...])
    inner = lax.broadcasted_iota(jnp.int32, (N, HALF), 1) != 0
    row = lax.broadcasted_iota(jnp.int32, (ROWS, N), 0)
    sign = jnp.where(lax.broadcasted_iota(jnp.int32, (ROWS, N), 1) % 2 == 0, 1.0 / 16.0, -1.0 / 16.0)

    def plane(p, carry):
        zz, b = p // 4, p % 4
        field = split(phi[zz, b])
        rows = split(product(field, (wh[...], wl[...])))
        u = product(cos, rows)
        v = product(sin, rows)
        re = u[:, :HALF] + jnp.where(inner, v[:, HALF:], 0.0)
        im = jnp.where(inner, u[:, HALF:], 0.0) - v[:, :HALF]
        for m in range(GX):
            out[m, pl.ds(zz * 32 + b, ROWS, stride=4), :] = re[ROWS * m : ROWS * (m + 1)]
            out[m, pl.ds(64 + zz * 32 + b, ROWS, stride=4), :] = im[ROWS * m : ROWS * (m + 1)]
        pick = jnp.where(row == p, sign, 0.0).astype(jnp.bfloat16)
        nt = (((1,), (1,)), ((), ()))
        edge[...] += lax.dot_general(
            pick, field[0], nt, preferred_element_type=jnp.float32
        ) + lax.dot_general(pick, field[1], nt, preferred_element_type=jnp.float32)
        return carry

    lax.fori_loop(0, 8, plane, 0)
    line = split(edge[...])
    line_re = product(line, cos)
    line_im = -product(line, sin)
    lane = lax.broadcasted_iota(jnp.int32, (ROWS, HALF), 1)
    for m in range(GX):
        at, off = HALF * (m // 16), 8 * (m % 16)
        re, im = line_re[:, at : at + HALF], line_im[:, at : at + HALF]
        tile = jnp.where(lane < 8, pltpu.roll(re, (HALF - off) % HALF, 1), 0.0)
        tile = jnp.where((lane >= 8) & (lane < 16), pltpu.roll(re, (HALF + 8 - off) % HALF, 1), tile)
        tile = jnp.where((lane >= 64) & (lane < 72), pltpu.roll(im, (HALF + 64 - off) % HALF, 1), tile)
        tile = jnp.where((lane >= 72) & (lane < 80), pltpu.roll(im, (HALF + 72 - off) % HALF, 1), tile)
        out[m, 128:136, :] = tile


def inverse_kernel(back, coeff, wh, wl, ch, cl, sh, sl, out):
    cos, sin = (ch[...], cl[...]), (sh[...], sl[...])

    def plane(p, carry):
        zz, b = p // 4, p % 4
        re = [back[m, pl.ds(zz * 32 + b, ROWS, stride=4), :] for m in range(GX)]
        im = [back[m, pl.ds(64 + zz * 32 + b, ROWS, stride=4), :] for m in range(GX)]
        modes = split(jnp.concatenate([jnp.concatenate(re, axis=0), jnp.concatenate(im, axis=0)], axis=1))
        u = product(cos, modes)
        v = product(sin, modes)
        rows = jnp.concatenate([u[:, :HALF] - v[:, HALF:], u[:, HALF:] + v[:, :HALF]], axis=1)
        out[zz, b] = product(split(rows), (wh[...], wl[...])) * coeff[zz]
        return carry

    lax.fori_loop(0, 8, plane, 0)


def exchange_kernel(src, dst, own, send, recv):
    me, ba = lax.axis_index("gx"), lax.axis_index("ba")
    barrier = pltpu.get_barrier_semaphore()

    def greet(k, carry):
        pl.semaphore_signal(barrier, inc=1, device_id=(lax.rem(me + k, GX), ba), device_id_type=MESH)
        return carry

    lax.fori_loop(1, GX, greet, 0)
    pl.semaphore_wait(barrier, GX - 1)
    mine = pltpu.make_async_copy(src.at[me], dst.at[me], own)
    mine.start()

    def copy(k):
        to = lax.rem(me + k, GX)
        return pltpu.make_async_remote_copy(
            src_ref=src.at[to],
            dst_ref=dst.at[me],
            send_sem=send.at[k],
            recv_sem=recv.at[k],
            device_id=(to, ba),
            device_id_type=MESH,
        )

    def start(k, carry):
        copy(k).start()
        return carry

    def finish(k, carry):
        copy(k).wait()
        return carry

    lax.fori_loop(1, GX, start, 0)
    lax.fori_loop(1, GX, finish, 0)
    mine.wait()


def exchange(value, ident):
    return pl.pallas_call(
        exchange_kernel,
        out_shape=jax.ShapeDtypeStruct(value.shape, value.dtype),
        in_specs=[pl.BlockSpec(memory_space=pl.ANY)],
        out_specs=pl.BlockSpec(memory_space=pl.ANY),
        scratch_shapes=[
            pltpu.SemaphoreType.DMA,
            pltpu.SemaphoreType.DMA((GX,)),
            pltpu.SemaphoreType.DMA((GX,)),
        ],
        compiler_params=pltpu.CompilerParams(collective_id=ident, has_side_effects=True),
        name="exchange" + str(ident),
    )(value)


def solve_kernel(spec, goal, edge_goal, alpha, bands, back, grads, acc, espec, enew, flux, others, send, recv):
    gx, ba = lax.axis_index("gx"), lax.axis_index("ba")
    barrier = pltpu.get_barrier_semaphore()
    for k in range(1, BA):
        pl.semaphore_signal(barrier, inc=1, device_id=(gx, lax.rem(ba + k, BA)), device_id_type=MESH)
    sub = lax.broadcasted_iota(jnp.int32, (ROWS, HALF), 0)
    lane = lax.broadcasted_iota(jnp.int32, (ROWS, HALF), 1)
    upper = sub < 4
    rate, speed, share = bands[0], bands[1], bands[2]
    couple = [speed * float(abs(COS[d])) for d in range(6)]

    def clear(z, carry):
        for d in range(12):
            acc[z, d] = jnp.zeros((ROWS, HALF), jnp.float32)
        return carry

    lax.fori_loop(0, 64, clear, 0)

    def gather(src, carry):
        line = spec[src, 16]
        for zz in range(2):
            col = line if zz == 0 else pltpu.roll(line, 4, 0)
            col_re = jnp.where(lane < 16, col, 0.0)
            col_im = jnp.where(lane < 16, pltpu.roll(col, 64, 1), 0.0)
            espec[src, zz] = jnp.where(upper, col_re, pltpu.roll(spec[src, zz * 4], 4, 0))
            espec[src, 2 + zz] = jnp.where(upper, col_im, pltpu.roll(spec[src, 8 + zz * 4], 4, 0))
        return carry

    lax.fori_loop(0, GX, gather, 0)

    def sweep(t, edge, first, start_re, start_im):
        at = 4 if edge else t
        inv = [(alpha[at, first + d, 0], alpha[at, first + d, 1]) for d in range(6)]

        def cells(step, psi):
            src = (GX - 1 - step) if first == 0 else step
            psi = list(psi)
            for zz in (1, 0) if first == 0 else (0, 1):
                z = 2 * src + zz
                if edge:
                    s_re, s_im = espec[src, zz], espec[src, 2 + zz]
                    g = [jnp.where(upper, edge_goal[z, 2 * c : 2 * c + 1], edge_goal[z, 2 * c + 1 : 2 * c + 2]) for c in range(2)]
                else:
                    s_re, s_im = spec[src, zz * 4 + t], spec[src, 8 + zz * 4 + t]
                    g = [
                        jnp.where(upper, goal[z, c, pl.ds(2 * t, 1), :], goal[z, c, pl.ds(2 * t + 1, 1), :])
                        for c in range(2)
                    ]
                s_re, s_im = s_re * rate, s_im * rate
                sum_re = sum_im = None
                for d in range(6):
                    t_re = s_re + couple[d] * psi[2 * d]
                    t_im = s_im + couple[d] * psi[2 * d + 1]
                    p_re = inv[d][0] * t_re - inv[d][1] * t_im
                    p_im = inv[d][0] * t_im + inv[d][1] * t_re
                    psi[2 * d], psi[2 * d + 1] = p_re, p_im
                    sum_re = p_re if d == 0 else sum_re + p_re
                    sum_im = p_im if d == 0 else sum_im + p_im
                    acc[z, first + d] += p_re * g[0] + p_im * g[1]
                if first == 0:
                    if edge:
                        enew[src, zz], enew[src, 2 + zz] = sum_re, sum_im
                    else:
                        back[src, zz * 4 + t], back[src, 8 + zz * 4 + t] = sum_re, sum_im
                elif not edge:
                    back[src, zz * 4 + t] = (back[src, zz * 4 + t] + sum_re) * (1.0 / 12.0)
                    back[src, 8 + zz * 4 + t] = (back[src, 8 + zz * 4 + t] + sum_im) * (1.0 / 12.0)
                else:
                    close(src, zz, (enew[src, zz] + sum_re) * (1.0 / 12.0), (enew[src, 2 + zz] + sum_im) * (1.0 / 12.0))
            return tuple(psi)

        return lax.fori_loop(0, GX, cells, tuple([start_re, start_im] * 6))

    mean = jnp.where(upper & (gx == HALF // ROWS), 0.5, 0.0)

    def close(src, zz, e_re, e_im):
        packed = []
        for c, e in ((0, e_re), (1, e_im)):
            at = 8 * c + zz * 4
            first = back[src, at]
            back[src, at] = first + mean * (pltpu.roll(e, 4, 0) - first)
            h = 0.5 * (e + pltpu.roll(e, HALF - 8, 1))
            packed.append(jnp.where(upper, h, pltpu.roll(pltpu.roll(h, 4, 0), HALF - 1, 1)))
        for t in range(4):
            x_re, x_im = [jnp.where(lane == 0, v if t == 0 else pltpu.roll(v, HALF - 2 * t, 1), 0.0) for v in packed]
            back[src, zz * 4 + t] = back[src, zz * 4 + t] - x_im
            back[src, 8 + zz * 4 + t] = back[src, 8 + zz * 4 + t] + x_re

    def absorbed(psi):
        parts = []
        for c in range(2):
            total = psi[c] * float(abs(COS[0]) / 12.0)
            for d in range(1, 6):
                total = total + psi[2 * d + c] * float(abs(COS[d]) / 12.0)
            parts.append(total)
        return parts

    zero = jnp.zeros((ROWS, HALF), jnp.float32)

    def down(t, carry):
        flux[2 * t], flux[2 * t + 1] = absorbed(sweep(t, False, 0, zero, zero))
        return carry

    flux[8], flux[9] = absorbed(sweep(0, True, 0, zero, zero))
    lax.fori_loop(0, 4, down, 0)

    pl.semaphore_wait(barrier, BA - 1)
    copies = []
    for k in range(1, BA):
        copies.append(
            pltpu.make_async_remote_copy(
                src_ref=flux,
                dst_ref=others.at[k - 1],
                send_sem=send.at[k - 1],
                recv_sem=recv.at[k - 1],
                device_id=(gx, lax.rem(ba + k, BA)),
                device_id_type=MESH,
            )
        )
        copies[-1].start()
    for copy in copies:
        copy.wait()

    odd, second = sub % 2 == 1, sub % 4 >= 2

    def wall(at):
        total = flux[at] + others[0, at] + others[1, at] + others[2, at]
        total = total + jnp.where(odd, pltpu.roll(total, 1, 0), pltpu.roll(total, ROWS - 1, 0))
        total = total + jnp.where(second, pltpu.roll(total, 2, 0), pltpu.roll(total, ROWS - 2, 0))
        return total * share

    def up(t, carry):
        sweep(t, False, 6, wall(2 * t), wall(2 * t + 1))
        return carry

    lax.fori_loop(0, 4, up, 0)
    sweep(0, True, 6, wall(8), wall(9))

    def reduce(src, carry):
        tile = jnp.zeros((ROWS, HALF), jnp.float32)
        for zz in range(2):
            for d in range(12):
                total = jnp.sum(acc[2 * src + zz, d], axis=1, keepdims=True)
                tile = jnp.where(lane == zz * 12 + d, total, tile)
        grads[src] = tile * (1.0 / N)
        return carry

    lax.fori_loop(0, GX, reduce, 0)


def vmem(count):
    return [pl.BlockSpec(memory_space=pltpu.VMEM)] * count


def solve(spec, goal, edge_goal, alpha, bands):
    f32 = jnp.float32
    return pl.pallas_call(
        solve_kernel,
        out_shape=[jax.ShapeDtypeStruct((GX, 16, ROWS, HALF), f32), jax.ShapeDtypeStruct((GX, ROWS, HALF), f32)],
        in_specs=vmem(5),
        out_specs=vmem(2),
        scratch_shapes=[
            pltpu.VMEM((64, 12, ROWS, HALF), f32),
            pltpu.VMEM((GX, 4, ROWS, HALF), f32),
            pltpu.VMEM((GX, 4, ROWS, HALF), f32),
            pltpu.VMEM((10, ROWS, HALF), f32),
            pltpu.VMEM((3, 10, ROWS, HALF), f32),
            pltpu.SemaphoreType.DMA((3,)),
            pltpu.SemaphoreType.DMA((3,)),
        ],
        compiler_params=pltpu.CompilerParams(collective_id=5, has_side_effects=True, vmem_limit_bytes=40 << 20),
        name="solve",
    )(spec, goal, edge_goal, alpha, bands)


def forward_transform(phi, rows, cos, sin):
    return pl.pallas_call(
        forward_kernel,
        out_shape=jax.ShapeDtypeStruct((GX, 136, HALF), jnp.float32),
        in_specs=vmem(7),
        out_specs=vmem(1)[0],
        scratch_shapes=[pltpu.VMEM((ROWS, N), jnp.float32)],
        compiler_params=pltpu.CompilerParams(vmem_limit_bytes=40 << 20),
        name="transform",
    )(phi, *rows, *cos, *sin)


def inverse_transform(back, coeff, rows, cos, sin):
    return pl.pallas_call(
        inverse_kernel,
        out_shape=jax.ShapeDtypeStruct((2, 4, N, N), jnp.float32),
        in_specs=vmem(8),
        out_specs=vmem(1)[0],
        compiler_params=pltpu.CompilerParams(vmem_limit_bytes=40 << 20),
        name="inverse",
    )(back, coeff, *rows, *cos, *sin)


def signed(index):
    return ((index + HALF) % N - HALF).astype(jnp.float32) * BASE


def propagators(rates, speeds, gx):
    sub = jnp.arange(ROWS)[:, None]
    lane = jnp.arange(HALF)[None, :]
    rate, speed = jnp.tile(rates, 2)[:, None], jnp.tile(speeds, 2)[:, None]
    fx, fy = [], []
    for t in range(4):
        fx.append(jnp.broadcast_to(signed(gx * ROWS + 2 * t + sub // 4), (ROWS, HALF)))
        fy.append(jnp.broadcast_to(signed(lane), (ROWS, HALF)))
    kx = gx * ROWS + lane % ROWS
    line = signed(kx)
    line = jnp.where((lane >= 8) & (kx == HALF), -line, line)
    fx.append(jnp.where(sub < 4, line, HALF * BASE))
    fy.append(jnp.where(sub < 4, jnp.where(lane < 8, -HALF * BASE, HALF * BASE), signed(lane)))
    fx, fy = jnp.stack(fx)[:, None], jnp.stack(fy)[:, None]
    sx, sy = jnp.asarray(SX, jnp.float32)[None, :, None, None], jnp.asarray(SY, jnp.float32)[None, :, None, None]
    wave = speed * (sx * fx + sy * fy)
    real = rate + jnp.asarray(np.abs(COS), jnp.float32)[None, :, None, None] * speed
    denom = real * real + wave * wave
    return jnp.stack([real / denom, -wave / denom], axis=2)


def targets(forward, gx):
    low = forward[..., :HALF]
    turned = jnp.flip(jnp.roll(forward, -1, axis=4)[..., HALF:], axis=4)
    ba_free = [(i, GX - 1 - i) for i in range(GX)]
    block = lax.ppermute(jnp.flip(jnp.roll(turned, -1, axis=3), axis=3), "gx", ba_free)
    lead = lax.ppermute(turned[:, :, :, :1], "gx", [(i, (GX - i) % GX) for i in range(GX)])
    mirror = jnp.concatenate([lead, block[:, :, :, 1:]], axis=3)
    lane = jnp.arange(HALF)[None, :]
    kx = gx * ROWS + jnp.arange(ROWS)[:, None]
    mirror = jnp.where((lane > 0) & (kx != HALF), mirror, 0.0)
    sign = jnp.array([1.0, -1.0], jnp.float32).reshape(1, 2, 1, 1, 1)
    goal = jnp.swapaxes(low + sign * mirror, 1, 2)
    own = jnp.where((lane > 0) & (gx == HALF // ROWS), turned[:, :, :, 0] * sign[..., 0], 0.0)
    line = jnp.pad(forward[..., HALF], ((0, 0), (0, 0), (0, 0), (0, HALF - ROWS)))
    edge = jnp.stack([line, own], axis=3)
    edge = jnp.swapaxes(edge, 1, 2).reshape(forward.shape[0], 64, 4, HALF)
    return goal, edge


def body(phi_start, coeff, forward, rates, speeds, shares):
    rows, inv_rows, cos, sin = tables()
    gx = lax.axis_index("gx")
    goal, edge = targets(forward, gx)
    alpha = propagators(rates, speeds, gx)
    bands = jnp.broadcast_to(jnp.tile(jnp.stack([rates, speeds, shares]), (1, 2))[:, :, None], (3, ROWS, HALF))
    phi = phi_start
    total = None
    for step in range(forward.shape[0]):
        spec = exchange(forward_transform(phi, rows, cos, sin), 1)
        back, grads = solve(spec.reshape(GX, 17, ROWS, HALF), goal[step], edge[step], alpha, bands)
        total = grads if step == 0 else total + grads
        back = exchange(back.reshape(GX, 128, HALF), 2)
        phi = inverse_transform(back, coeff, inv_rows, cos, sin)
    parts = jnp.sum(exchange(total, 3), axis=0)[:, :24].reshape(2, 4, 2, 12)
    return (phi, jnp.transpose(parts[0] + parts[1], (1, 2, 0)))


def solution(mesh):
    in_specs = (
        P("gx", "ba", None, None),
        P("gx", None, None),
        P(None, None, None, "gx", None),
        P("ba"),
        P("ba"),
        P("ba"),
    )
    out_specs = (P("gx", "ba", None, None), P("gx", None, "ba"))
    return jax.shard_map(body, mesh=mesh, in_specs=in_specs, out_specs=out_specs, check_vma=False)
```

profile of v0, /device:TPU:1, one launch (start us, length us, event | category | flops | bytes accessed | tf_op | source)
XLA Modules:
  0.0 285.4 jit_solution(11861569004478796673)
XLA Ops:
  0.6 2.3 slice.62
  3.0 1.1 fusion.30
  4.6 1.3 slice.65
  5.9 7.6 %collective-permute-start = (f32[2,2,64,1,128]{4,3,1,2,0:T(1,128)}, f32[2,2,64,1,128]{4,3,1,2,0:T(1,128)}, u32[]{:S(2)}, u32[]{:S(2)}) collective-permute-start(f32[2,2,64,1,128]{4,3,1,2,0:T(1,128)} %slice.65), channel_id=1, source_target_pairs={{0,0},{4,124},{8,120},{12,116},{16,112},{20,108},{24,104},{28,100}... | collective-permute-start | bytes 393224 | tf_op jit(solution)/shard_map/ppermute | solution.py:408
  14.5 1.1 pad_maximum_fusion.1
  15.7 1.1 rev.6
  16.9 1.7 collective-permute-start.1
  19.0 2.8 copy.28
  22.1 1.1 broadcast_select_fusion
  24.3 0.9 fusion.3
  25.4 6.1 %transform.2.src = f32[32,136,128]{2,1,0:T(8,128)S(1)} custom-call(f32[2,4,256,256]{3,2,1,0:T(8,128)S(1)} %copy-done.10, bf16[256,256]{1,0:T(8,128)(2,1)S(1)} %copy-done.17, bf16[256,256]{1,0:T(8,128)(2,1)S(1)} %copy-done.16, bf16[256,256]{1,0:T(8,128)(2,1)S(1)} %copy-done.9, bf16[256,256]{1,0:T(8,128)(2,1)S(1)} %copy-done.8, ...), custom_call_target="tpu_custom_call" | custom-call | tf_op jit(solution)/shard_map/transform/pallas_call | solution.py:356
  31.5 1.4 copy-done.1
  32.9 40.4 %exchange1.2 = f32[32,136,128]{2,1,0:T(8,128)} custom-call(f32[32,136,128]{2,1,0:T(8,128)} %copy-done.1), custom_call_target="tpu_custom_call" | custom-call | tf_op jit(solution)/shard_map/exchange1/pallas_call | solution.py:165
  73.4 1.2 pad_maximum_fusion.2.alpha
  74.6 1.3 slice.76
  76.0 1.3 fusion.2
  77.6 30.1 %solve.2 = (f32[32,16,8,128]{3,2,1,0:T(8,128)S(1)}, f32[32,8,128]{2,1,0:T(8,128)S(1)}) custom-call(f32[32,17,8,128]{3,2,1,0:T(8,128)S(1)} %bitcast.20, f32[64,2,8,128]{3,2,1,0:T(8,128)S(1)} %get-tuple-element.15.goal, f32[64,4,128]{2,1,0:T(4,128)S(1)} %bitcast.25, f32[5,12,2,8,128]{4,3,2,1,0:T(8,128)S(1)} %pad_maximum_fusion.2.alpha, ...), custom_call_target="tpu_custom_call" | custom-call | tf_op jit(solution)/shard_map/solve/pallas_call | solution.py:336
  107.8 1.3 copy-done.12
  109.1 36.9 %exchange2.2.back = f32[32,128,128]{2,1,0:T(8,128)} custom-call(f32[32,128,128]{2,1,0:T(8,128)} %bitcast.23), custom_call_target="tpu_custom_call" | custom-call | tf_op jit(solution)/shard_map/exchange2/pallas_call | solution.py:165
  146.0 1.6 copy-done.5
  147.6 6.0 %inverse.2.phi = f32[2,4,256,256]{3,2,1,0:T(8,128)S(1)} custom-call(f32[32,128,128]{2,1,0:T(8,128)S(1)} %copy-done.5, f32[2,256,256]{2,1,0:T(8,128)S(1)} %copy-done.13, bf16[256,256]{1,0:T(8,128)(2,1)S(1)} %copy-done.15, bf16[256,256]{1,0:T(8,128)(2,1)S(1)} %copy-done.14, bf16[256,256]{1,0:T(8,128)(2,1)S(1)} %copy-done.9, bf16[256,256]{1,0:T(8,128)(2,1)S(1)} %copy-done.8, ...), custom_call_target="tpu_custom_call" | custom-call | tf_op jit(solution)/shard_map/inverse/pallas_call | solution.py:368
  153.6 6.1 %transform.3.src = f32[32,136,128]{2,1,0:T(8,128)S(1)} custom-call(f32[2,4,256,256]{3,2,1,0:T(8,128)S(1)} %inverse.2.phi, bf16[256,256]{1,0:T(8,128)(2,1)S(1)} %copy-done.17, bf16[256,256]{1,0:T(8,128)(2,1)S(1)} %copy-done.16, bf16[256,256]{1,0:T(8,128)(2,1)S(1)} %copy-done.9, bf16[256,256]{1,0:T(8,128)(2,1)S(1)} %copy-done.8, ...), custom_call_target="tpu_custom_call" | custom-call | tf_op jit(solution)/shard_map/transform/pallas_call | solution.py:356
  159.7 1.4 copy-done
  161.1 38.3 %exchange1.3 = f32[32,136,128]{2,1,0:T(8,128)} custom-call(f32[32,136,128]{2,1,0:T(8,128)} %copy-done), custom_call_target="tpu_custom_call" | custom-call | tf_op jit(solution)/shard_map/exchange1/pallas_call | solution.py:165
  199.3 1.6 copy-done.3
  200.9 27.6 %solve.3 = (f32[32,16,8,128]{3,2,1,0:T(8,128)S(1)}, f32[32,8,128]{2,1,0:T(8,128)S(1)}) custom-call(f32[32,17,8,128]{3,2,1,0:T(8,128)S(1)} %bitcast.21, f32[64,2,8,128]{3,2,1,0:T(8,128)S(1)} %get-tuple-element.14.goal, f32[64,4,128]{2,1,0:T(4,128)S(1)} %bitcast.24, f32[5,12,2,8,128]{4,3,2,1,0:T(8,128)S(1)} %pad_maximum_fusion.2.alpha, ...), custom_call_target="tpu_custom_call" | custom-call | tf_op jit(solution)/shard_map/solve/pallas_call | solution.py:336
  228.5 1.3 copy-done.11
  229.8 35.6 %exchange2.3.back = f32[32,128,128]{2,1,0:T(8,128)} custom-call(f32[32,128,128]{2,1,0:T(8,128)} %bitcast.22), custom_call_target="tpu_custom_call" | custom-call | tf_op jit(solution)/shard_map/exchange2/pallas_call | solution.py:165
  265.4 1.6 copy-done.4
  267.0 7.3 %inverse.3 = f32[2,4,256,256]{3,2,1,0:T(8,128)} custom-call(f32[32,128,128]{2,1,0:T(8,128)S(1)} %copy-done.4, f32[2,256,256]{2,1,0:T(8,128)S(1)} %copy-done.13, bf16[256,256]{1,0:T(8,128)(2,1)S(1)} %copy-done.15, bf16[256,256]{1,0:T(8,128)(2,1)S(1)} %copy-done.14, bf16[256,256]{1,0:T(8,128)(2,1)S(1)} %copy-done.9, bf16[256,256]{1,0:T(8,128)(2,1)S(1)} %copy-done.8, ...), custom_call_target="tpu_custom_call" | custom-call | tf_op jit(solution)/shard_map/inverse/pallas_call | solution.py:368
  274.9 8.8 %exchange3.1 = f32[32,8,128]{2,1,0:T(8,128)} custom-call(f32[32,8,128]{2,1,0:T(8,128)} %add.349.src), custom_call_target="tpu_custom_call" | custom-call | tf_op jit(solution)/shard_map/exchange3/pallas_call | solution.py:165
  283.8 0.9 reduce_sum.9
  (92 shorter events, 5.0 us)
Async XLA Ops:
  0.6 2.4 copy-start.19
  5.9 70.1 %collective-permute-start = (f32[2,2,64,1,128]{4,3,1,2,0:T(1,128)}, f32[2,2,64,1,128]{4,3,1,2,0:T(1,128)}, u32[]{:S(2)}, u32[]{:S(2)}) collective-permute-start(f32[2,2,64,1,128]{4,3,1,2,0:T(1,128)} %slice.65), channel_id=1, source_target_pairs={{0,0},{4,124},{8,120},{12,116},{16,112},{20,108},{24,104},{28,100}... | collective-permute-start | bytes 393224 | tf_op jit(solution)/shard_map/ppermute | solution.py:408
  14.5 4.3 %copy-start.25 = (f32[4]{0:T(128)S(1)}, f32[4]{0:T(128)}, u32[]{:S(2)}) copy-start(f32[4]{0:T(128)} %param.21) | copy-start | bytes 52
  14.5 4.4 %copy-start.24 = (f32[4]{0:T(128)S(1)}, f32[4]{0:T(128)}, u32[]{:S(2)}) copy-start(f32[4]{0:T(128)} %param.22) | copy-start | bytes 52
  15.6 6.5 %copy-start.21 = (f32[2]{0:T(128)S(1)}, f32[2]{0:T(128)}, u32[]{:S(2)}) copy-start(f32[2]{0:T(128)} %constant.164.clone) | copy-start | bytes 28
  15.6 8.0 %copy-start.27 = (f32[12]{0:T(128)S(1)}, f32[12]{0:T(128)}, u32[]{:S(2)}) copy-start(f32[12]{0:T(128)} %constant.167.clone) | copy-start | bytes 148
  15.6 8.7 %copy-start.22 = (f32[12]{0:T(128)S(1)}, f32[12]{0:T(128)}, u32[]{:S(2)}) copy-start(f32[12]{0:T(128)} %constant.166.clone) | copy-start | bytes 148
  15.6 8.7 %copy-start.23 = (f32[12]{0:T(128)S(1)}, f32[12]{0:T(128)}, u32[]{:S(2)}) copy-start(f32[12]{0:T(128)} %constant.165.clone) | copy-start | bytes 148
  16.8 8.5 %copy-start.26 = (f32[4]{0:T(128)S(1)}, f32[4]{0:T(128)}, u32[]{:S(2)}) copy-start(f32[4]{0:T(128)} %param.23) | copy-start | bytes 52
  16.8 8.6 %copy-start.6 = (bf16[256,256]{1,0:T(8,128)(2,1)S(1)}, bf16[256,256]{1,0:T(8,128)(2,1)}, u32[]{:S(2)}) copy-start(bf16[256,256]{1,0:T(8,128)(2,1)} %constant.163.clone.sl) | copy-start | bytes 393220
  16.8 8.6 %copy-start.7 = (bf16[256,256]{1,0:T(8,128)(2,1)S(1)}, bf16[256,256]{1,0:T(8,128)(2,1)}, u32[]{:S(2)}) copy-start(bf16[256,256]{1,0:T(8,128)(2,1)} %constant.162.clone.sh) | copy-start | bytes 393220
  16.8 8.6 %copy-start.8 = (bf16[256,256]{1,0:T(8,128)(2,1)S(1)}, bf16[256,256]{1,0:T(8,128)(2,1)}, u32[]{:S(2)}) copy-start(bf16[256,256]{1,0:T(8,128)(2,1)} %constant.161.clone.cl) | copy-start | bytes 393220
  16.8 8.6 %copy-start.9 = (bf16[256,256]{1,0:T(8,128)(2,1)S(1)}, bf16[256,256]{1,0:T(8,128)(2,1)}, u32[]{:S(2)}) copy-start(bf16[256,256]{1,0:T(8,128)(2,1)} %constant.160.clone.ch) | copy-start | bytes 393220
  16.8 8.6 %copy-start.10 = (f32[2,4,256,256]{3,2,1,0:T(8,128)S(1)}, f32[2,4,256,256]{3,2,1,0:T(8,128)}, u32[]{:S(2)}) copy-start(f32[2,4,256,256]{3,2,1,0:T(8,128)} %phi.1) | copy-start | bytes 6291460
  16.8 8.6 %copy-start.16 = (bf16[256,256]{1,0:T(8,128)(2,1)S(1)}, bf16[256,256]{1,0:T(8,128)(2,1)}, u32[]{:S(2)}) copy-start(bf16[256,256]{1,0:T(8,128)(2,1)} %constant.157.clone.wl) | copy-start | bytes 393220
  16.8 8.6 %copy-start.17 = (bf16[256,256]{1,0:T(8,128)(2,1)S(1)}, bf16[256,256]{1,0:T(8,128)(2,1)}, u32[]{:S(2)}) copy-start(bf16[256,256]{1,0:T(8,128)(2,1)} %constant.156.clone.wh) | copy-start | bytes 393220
  16.9 57.8 %collective-permute-start.1 = (f32[2,2,64,8,128]{4,3,1,2,0:T(8,128)}, f32[2,2,64,8,128]{4,3,1,2,0:T(8,128)}, u32[]{:S(2)}, u32[]{:S(2)}) collective-permute-start(f32[2,2,64,8,128]{4,3,1,2,0:T(8,128)} %rev.6), channel_id=1, source_target_pairs={{0,124},{4,120},{8,116},{12,112},{16,108},{20,104},{24,100},{28,96... | collective-permute-start | bytes 3145736 | tf_op jit(solution)/shard_map/ppermute | solution.py:407
  31.5 1.4 copy-start.1
  73.4 2.6 copy-start.20
  76.0 1.7 copy-start.2
  76.0 1.7 copy-start.18
  107.8 1.3 copy-start.12
  109.1 36.9 %copy-start.13 = (f32[2,256,256]{2,1,0:T(8,128)S(1)}, f32[2,256,256]{2,1,0:T(8,128)}, u32[]{:S(2)}) copy-start(f32[2,256,256]{2,1,0:T(8,128)} %coeff.3) | copy-start | bytes 1572868
  109.1 36.9 %copy-start.14 = (bf16[256,256]{1,0:T(8,128)(2,1)S(1)}, bf16[256,256]{1,0:T(8,128)(2,1)}, u32[]{:S(2)}) copy-start(bf16[256,256]{1,0:T(8,128)(2,1)} %constant.159.clone.wl) | copy-start | bytes 393220
  109.1 36.9 %copy-start.15 = (bf16[256,256]{1,0:T(8,128)(2,1)S(1)}, bf16[256,256]{1,0:T(8,128)(2,1)}, u32[]{:S(2)}) copy-start(bf16[256,256]{1,0:T(8,128)(2,1)} %constant.158.clone.wh) | copy-start | bytes 393220
  146.0 1.6 copy-start.5
  159.7 1.4 copy-start
  199.3 1.6 copy-start.3
  228.5 1.3 copy-start.11
  265.4 1.6 copy-start.4
where the time goes:
time: 286 us; the launch traced here: 285 us
  Pallas kernels  243 us (85%)
  local copies, waits for them, and re-layouts  23.3 us (8%)
  starting transfers between devices  9.35 us (3%)
  other arithmetic  8.6 us (3%)
    pallas_call x5, Pallas kernels, exchange(): pl.pallas_call(exchange_kernel, out_shape=jax.ShapeDtypeStruct(value.shap...  160 us
    pallas_call x2, Pallas kernels, solve(): pl.pallas_call(solve_kernel, out_shape=[jax.ShapeDtypeStruct((GX, 16, ROW...  57.7 us
    unnamed x67, local copies, waits for them, and re-layouts  14.3 us
    pallas_call x2, Pallas kernels, inverse_transform(): pl.pallas_call(inverse_kernel, out_shape=jax.ShapeDtypeStruct((2, 4, N, N...  13.2 us
    pallas_call x2, Pallas kernels, forward_transform(): pl.pallas_call(forward_kernel, out_shape=jax.ShapeDtypeStruct((GX, 136, H...  12.2 us
    ppermute x1, starting transfers between devices, targets(): lax.ppermute(turned[:, :, :, :1], 'gx', [(i, (GX - i) % GX) for i in rang...  7.64 us
  transfers between devices with their start and end apart: 2, of which 0 were waited for; matrix products, arithmetic and copies ran while one was open for 4% of the time, Pallas kernels for 16%

commit v1 on v0

v1 whole, which is shorter than its diff:
```python
import functools
import math

import jax
import jax.numpy as jnp
import numpy as np
from jax import lax
from jax.experimental import pallas as pl
from jax.experimental.pallas import tpu as pltpu
from jax.sharding import PartitionSpec as P

MESH = pl.DeviceIdType.MESH
N = 256
HALF = 128
GX = 32
BA = 4
ROWS = 8
BASE = 1.5 * 2.0 * math.pi / N


def quadrature():
    level = np.arange(6)
    polar = 0.2 + 0.15 * level
    cosine = np.concatenate([-polar, polar])
    azimuth = np.concatenate([level * (math.pi / 3.0) + math.pi / 6.0, level * (math.pi / 3.0)])
    sine = np.sqrt(1.0 - cosine * cosine)
    return cosine, sine * np.cos(azimuth), sine * np.sin(azimuth)


COS, SX, SY = quadrature()


def halves(table):
    table = jnp.asarray(table, jnp.float32)
    high = table.astype(jnp.bfloat16)
    return high, (table - high.astype(jnp.float32)).astype(jnp.bfloat16)


def np_halves(table):
    table = np.asarray(table, np.float32)
    high = table.astype(jnp.bfloat16)
    low = (table - high.astype(np.float32)).astype(jnp.bfloat16)
    return [jnp.asarray(high), jnp.asarray(low)]


def tables():
    index = np.arange(N)
    angle = (index[:, None] * index[None, :] % N) * (2.0 * np.pi / N)
    cos, sin = np.cos(angle) / 16.0, np.sin(angle) / 16.0
    rows = np.concatenate([cos[:, :HALF], -sin[:, :HALF]], axis=1)
    rows[:, HALF] = cos[:, HALF]
    back = np.concatenate([2.0 * cos[:HALF], -2.0 * sin[:HALF]], axis=0)
    back[0] = cos[0]
    back[HALF] = cos[HALF]
    order = np.arange(N).reshape(GX, ROWS).T.reshape(-1)
    stacks = [rows, back, cos, sin, cos[order], sin[order], cos[:, order], sin[:, order]]
    return [part for stack in stacks for part in np_halves(stack)]


def split(value):
    high = value.astype(jnp.bfloat16)
    return high, (value - high.astype(jnp.float32)).astype(jnp.bfloat16)


def product(left, right):
    lh, ll = left
    rh, rl = right
    dot = functools.partial(jnp.dot, preferred_element_type=jnp.float32)
    return dot(lh, rh) + (dot(ll, rh) + dot(lh, rl))


SENT = 136
BACK = 128
OUTWARD = ((0, 2), (2, 3), (5, 4), (9, 4), (13, 4))
HOMEWARD = ((0, 4), (4, 4), (8, 4), (12, 4))
FLUXES = ((0, 4), (4, 2), (6, 2), (8, 2))
TABLES = 16


def spot(t, zz, part):
    return 4 * t + 2 * zz + part + (1 if t > 0 else 0)


def tile_of(ref, row):
    return ref[pl.ds(pl.multiple_of(row, ROWS), ROWS), :]


def kernel(phi, coeff_in, goal_in, edge_in, alpha, bands, *rest):
    names = [rest[2 * i : 2 * i + 2] for i in range(TABLES // 2)]
    wave_y, back_y, cos_x, sin_x, cos_rows, sin_rows, cos_cols, sin_cols = names
    (out, grads, field, coeff, goal, edge_goal, sent, spec, made, back, acc, espec, enew, epack, flux, others,
     gsum, gall, line_of, load, store, own, own_back, send, recv, send_back, recv_back, send_flux, recv_flux,
     send_grad, recv_grad) = rest[TABLES:]
    gx, ba = lax.axis_index("gx"), lax.axis_index("ba")
    barrier = pltpu.get_barrier_semaphore()

    def greet(k, carry):
        pl.semaphore_signal(barrier, inc=1, device_id=(lax.rem(gx + k, GX), ba), device_id_type=MESH)
        return carry

    lax.fori_loop(1, GX, greet, 0)
    for k in range(1, BA):
        pl.semaphore_signal(barrier, inc=1, device_id=(gx, lax.rem(ba + k, BA)), device_id_type=MESH)

    loads = [
        pltpu.make_async_copy(phi.at[0], field.at[0], load.at[0]),
        pltpu.make_async_copy(phi.at[1], field.at[1], load.at[1]),
        pltpu.make_async_copy(goal_in, goal, load.at[2]),
        pltpu.make_async_copy(edge_in, edge_goal, load.at[3]),
        pltpu.make_async_copy(coeff_in, coeff, load.at[4]),
    ]
    for copy in loads:
        copy.start()

    sub = lax.broadcasted_iota(jnp.int32, (ROWS, HALF), 0)
    lane = lax.broadcasted_iota(jnp.int32, (ROWS, HALF), 1)
    upper = sub < 4
    rate, speed, share = bands[0], bands[1], bands[2]
    couple = [speed * float(abs(COS[d])) for d in range(6)]
    zero = jnp.zeros((ROWS, HALF), jnp.float32)

    def clear(z, carry):
        for d in range(12):
            acc[z, d] = zero
        return carry

    lax.fori_loop(0, 64, clear, 0)

    def outward(message, k):
        first, count = OUTWARD[message]
        to = lax.rem(gx + k, GX)
        return pltpu.make_async_remote_copy(
            src_ref=sent.at[pl.ds(pl.multiple_of(to * SENT + first * ROWS, ROWS), count * ROWS), :],
            dst_ref=spec.at[pl.ds(pl.multiple_of(gx * SENT + first * ROWS, ROWS), count * ROWS), :],
            send_sem=send.at[message, k],
            recv_sem=recv.at[message, k],
            device_id=(to, ba),
            device_id_type=MESH,
        )

    def outward_own(message):
        first, count = OUTWARD[message]
        rows = pl.ds(pl.multiple_of(gx * SENT + first * ROWS, ROWS), count * ROWS)
        return pltpu.make_async_copy(sent.at[rows, :], spec.at[rows, :], own.at[message])

    def homeward(message, k):
        first, count = HOMEWARD[message]
        to = lax.rem(gx + k, GX)
        return pltpu.make_async_remote_copy(
            src_ref=made.at[pl.ds(pl.multiple_of(to * BACK + first * ROWS, ROWS), count * ROWS), :],
            dst_ref=back.at[pl.ds(pl.multiple_of(gx * BACK + first * ROWS, ROWS), count * ROWS), :],
            send_sem=send_back.at[message, k],
            recv_sem=recv_back.at[message, k],
            device_id=(to, ba),
            device_id_type=MESH,
        )

    def homeward_own(message):
        first, count = HOMEWARD[message]
        rows = pl.ds(pl.multiple_of(gx * BACK + first * ROWS, ROWS), count * ROWS)
        return pltpu.make_async_copy(made.at[rows, :], back.at[rows, :], own_back.at[message])

    def wall_copy(s, message, k):
        first, count = FLUXES[message]
        return pltpu.make_async_remote_copy(
            src_ref=flux.at[s, pl.ds(first, count)],
            dst_ref=others.at[s, k - 1, pl.ds(first, count)],
            send_sem=send_flux.at[s, message, k - 1],
            recv_sem=recv_flux.at[s, message, k - 1],
            device_id=(gx, lax.rem(ba + k, BA)),
            device_id_type=MESH,
        )

    def grad_copy(k):
        to = lax.rem(gx + k, GX)
        return pltpu.make_async_remote_copy(
            src_ref=gsum.at[to],
            dst_ref=gall.at[gx],
            send_sem=send_grad.at[k],
            recv_sem=recv_grad.at[k],
            device_id=(to, ba),
            device_id_type=MESH,
        )

    def over_peers(act):
        def one(k, carry):
            act(k)
            return carry

        lax.fori_loop(1, GX, one, 0)

    def start_outward(message):
        outward_own(message).start()
        over_peers(lambda k: outward(message, k).start())

    def wait_outward(message):
        outward_own(message).wait()
        over_peers(lambda k: outward(message, k).wait_recv())

    def start_homeward(message):
        homeward_own(message).start()
        over_peers(lambda k: homeward(message, k).start())

    def wait_homeward():
        for message in range(len(HOMEWARD)):
            homeward_own(message).wait()
            over_peers(lambda k: homeward(message, k).wait_recv())

    def sends_done(s):
        for message in range(len(OUTWARD)):
            over_peers(lambda k: outward(message, k).wait_send())
        for message in range(len(HOMEWARD)):
            over_peers(lambda k: homeward(message, k).wait_send())
        for message in range(len(FLUXES)):
            for k in range(1, BA):
                wall_copy(s, message, k).wait_send()

    inner = lax.broadcasted_iota(jnp.int32, (N, HALF), 1) != 0
    row8 = lax.broadcasted_iota(jnp.int32, (ROWS, N), 0)
    sign = jnp.where(lax.broadcasted_iota(jnp.int32, (ROWS, N), 1) % 2 == 0, 1.0 / 16.0, -1.0 / 16.0)

    def both(pair):
        return pair[0][...], pair[1][...]

    def forward(zz):
        def plane(b, carry):
            value = split(field[zz, b])
            rows = split(product(value, both(wave_y)))
            u = product(both(cos_rows), rows)
            v = product(both(sin_rows), rows)
            re = u[:, :HALF] + jnp.where(inner, v[:, HALF:], 0.0)
            im = jnp.where(inner, u[:, HALF:], 0.0) - v[:, :HALF]
            for t in range(4):
                for r in range(2):
                    for m in range(0, GX, ROWS):
                        at = (2 * t + r) * GX + m
                        for part, value_ in ((0, re), (1, im)):
                            row = m * SENT + spot(t, zz, part) * ROWS + r * 4
                            sent[pl.ds(row + b, ROWS, stride=SENT), :] = value_[at : at + ROWS]
            pick = jnp.where(row8 == zz * 4 + b, sign, 0.0).astype(jnp.bfloat16)
            nt = (((1,), (1,)), ((), ()))
            line_of[...] += lax.dot_general(
                pick, value[0], nt, preferred_element_type=jnp.float32
            ) + lax.dot_general(pick, value[1], nt, preferred_element_type=jnp.float32)
            return carry

        lax.fori_loop(0, 4, plane, 0)

    def edges():
        line = split(line_of[...])
        line_re = product(line, both(cos_x))
        line_im = -product(line, both(sin_x))
        for m in range(GX):
            at, off = HALF * (m // 16), 8 * (m % 16)
            re, im = line_re[:, at : at + HALF], line_im[:, at : at + HALF]
            tile = jnp.where(lane < 8, pltpu.roll(re, (HALF - off) % HALF, 1), 0.0)
            tile = jnp.where((lane >= 8) & (lane < 16), pltpu.roll(re, (HALF + 8 - off) % HALF, 1), tile)
            tile = jnp.where((lane >= 64) & (lane < 72), pltpu.roll(im, (HALF + 64 - off) % HALF, 1), tile)
            tile = jnp.where((lane >= 72) & (lane < 80), pltpu.roll(im, (HALF + 72 - off) % HALF, 1), tile)
            sent[m * SENT + 32 : m * SENT + 40, :] = tile

    def inverse(zz):
        def plane(b, carry):
            parts = []
            for part in range(2):
                pieces = []
                for t in range(4):
                    for r in range(2):
                        for m in range(0, GX, ROWS):
                            row = m * BACK + (4 * t + 2 * zz + part) * ROWS + r * 4
                            pieces.append(back[pl.ds(row + b, ROWS, stride=BACK), :])
                parts.append(jnp.concatenate(pieces, axis=0))
            modes = split(jnp.concatenate(parts, axis=1))
            u = product(both(cos_cols), modes)
            v = product(both(sin_cols), modes)
            rows = jnp.concatenate([u[:, :HALF] - v[:, HALF:], u[:, HALF:] + v[:, :HALF]], axis=1)
            field[zz, b] = product(split(rows), both(back_y)) * coeff[zz]
            return carry

        lax.fori_loop(0, 4, plane, 0)

    def gather():
        def one(src, carry):
            base = src * SENT
            line = tile_of(spec, base + 4 * ROWS)
            for zz in range(2):
                col = line if zz == 0 else pltpu.roll(line, 4, 0)
                col_re = jnp.where(lane < 16, col, 0.0)
                col_im = jnp.where(lane < 16, pltpu.roll(col, 64, 1), 0.0)
                espec[src, zz] = jnp.where(upper, col_re, pltpu.roll(tile_of(spec, base + spot(0, zz, 0) * ROWS), 4, 0))
                espec[src, 2 + zz] = jnp.where(
                    upper, col_im, pltpu.roll(tile_of(spec, base + spot(0, zz, 1) * ROWS), 4, 0)
                )
            return carry

        lax.fori_loop(0, GX, one, 0)

    mean = jnp.where(upper & (gx == HALF // ROWS), 0.5, 0.0)

    def sweep(s, t, first, start_re, start_im):
        edge = t == 4
        inv = [(alpha[t, first + d, 0], alpha[t, first + d, 1]) for d in range(6)]

        def cells(step, psi):
            src = (GX - 1 - step) if first == 0 else step
            psi = list(psi)
            for zz in (1, 0) if first == 0 else (0, 1):
                z = 2 * src + zz
                if edge:
                    s_re, s_im = espec[src, zz], espec[src, 2 + zz]
                    g = [
                        jnp.where(upper, edge_goal[s, z, 2 * c : 2 * c + 1], edge_goal[s, z, 2 * c + 1 : 2 * c + 2])
                        for c in range(2)
                    ]
                else:
                    s_re = tile_of(spec, src * SENT + spot(t, zz, 0) * ROWS)
                    s_im = tile_of(spec, src * SENT + spot(t, zz, 1) * ROWS)
                    g = [
                        jnp.where(upper, goal[s, z, c, 2 * t : 2 * t + 1], goal[s, z, c, 2 * t + 1 : 2 * t + 2])
                        for c in range(2)
                    ]
                s_re, s_im = s_re * rate, s_im * rate
                sums = [None, None]
                for d in range(6):
                    t_re = s_re + couple[d] * psi[2 * d]
                    t_im = s_im + couple[d] * psi[2 * d + 1]
                    p_re = inv[d][0] * t_re - inv[d][1] * t_im
                    p_im = inv[d][0] * t_im + inv[d][1] * t_re
                    psi[2 * d], psi[2 * d + 1] = p_re, p_im
                    sums = [p_re, p_im] if d == 0 else [sums[0] + p_re, sums[1] + p_im]
                    acc[z, first + d] += p_re * g[0] + p_im * g[1]
                if edge:
                    if first == 0:
                        enew[src, zz], enew[src, 2 + zz] = sums
                        continue
                    for c in range(2):
                        e = (enew[src, 2 * c + zz] + sums[c]) * (1.0 / 12.0)
                        enew[src, 2 * c + zz] = pltpu.roll(e, 4, 0)
                        h = 0.5 * (e + pltpu.roll(e, HALF - 8, 1))
                        epack[src, 2 * c + zz] = jnp.where(
                            upper, h, pltpu.roll(pltpu.roll(h, 4, 0), HALF - 1, 1)
                        )
                    continue
                for c in range(2):
                    rows = pl.ds(pl.multiple_of(src * BACK + (4 * t + 2 * zz + c) * ROWS, ROWS), ROWS)
                    if first == 0:
                        made[rows, :] = sums[c]
                        continue
                    total = (made[rows, :] + sums[c]) * (1.0 / 12.0)
                    if t == 0:
                        total = total + mean * (enew[src, 2 * c + zz] - total)
                    x = epack[src, 2 * (1 - c) + zz]
                    x = jnp.where(lane == 0, x if t == 0 else pltpu.roll(x, HALF - 2 * t, 1), 0.0)
                    made[rows, :] = total - x if c == 0 else total + x
            return tuple(psi)

        return lax.fori_loop(0, GX, cells, tuple([start_re, start_im] * 6))

    def down(s, t):
        psi = sweep(s, t, 0, zero, zero)
        at = 0 if t == 4 else 2 * t + 2
        for c in range(2):
            total = psi[c] * float(abs(COS[0]) / 12.0)
            for d in range(1, 6):
                total = total + psi[2 * d + c] * float(abs(COS[d]) / 12.0)
            flux[s, at + c] = total

    odd, second = sub % 2 == 1, sub % 4 >= 2

    def up(s, t):
        at = 0 if t == 4 else 2 * t + 2
        starts = []
        for c in range(2):
            total = flux[s, at + c] + others[s, 0, at + c] + others[s, 1, at + c] + others[s, 2, at + c]
            total = total + jnp.where(odd, pltpu.roll(total, 1, 0), pltpu.roll(total, ROWS - 1, 0))
            total = total + jnp.where(second, pltpu.roll(total, 2, 0), pltpu.roll(total, ROWS - 2, 0))
            starts.append(total * share)
        sweep(s, t, 6, *starts)

    def start_wall(s, message):
        for k in range(1, BA):
            wall_copy(s, message, k).start()

    def wait_wall(s, message):
        for k in range(1, BA):
            wall_copy(s, message, k).wait_recv()

    def one_step(s, carry):
        line_of[...] = jnp.zeros_like(line_of)

        @pl.when(s > 0)
        def _():
            wait_homeward()
            sends_done(s - 1)
            inverse(0)

        @pl.when(s == 0)
        def _():
            loads[0].wait()

        forward(0)

        @pl.when(s == 0)
        def _():
            pl.semaphore_wait(barrier, GX - 1 + BA - 1)

        start_outward(0)

        @pl.when(s > 0)
        def _():
            inverse(1)

        @pl.when(s == 0)
        def _():
            loads[1].wait()

        forward(1)
        edges()
        for message in range(1, len(OUTWARD)):
            start_outward(message)

        @pl.when(s == 0)
        def _():
            for copy in loads[2:]:
                copy.wait()

        wait_outward(0)
        wait_outward(1)
        gather()
        down(s, 4)
        down(s, 0)
        start_wall(s, 0)
        wait_outward(2)
        down(s, 1)
        start_wall(s, 1)
        wait_wall(s, 0)
        up(s, 4)
        up(s, 0)
        start_homeward(0)
        for t in (1, 2):
            wait_outward(t + 2)
            down(s, t + 1)
            start_wall(s, t + 1)
            wait_wall(s, t)
            up(s, t)
            start_homeward(t)
        wait_wall(s, 3)
        up(s, 3)
        start_homeward(3)
        return carry

    lax.fori_loop(0, 2, one_step, 0)

    def reduce(src, carry):
        tile = zero
        for zz in range(2):
            for d in range(12):
                total = jnp.sum(acc[2 * src + zz, d], axis=1, keepdims=True)
                tile = jnp.where(lane == zz * 12 + d, total, tile)
        gsum[src] = tile * (1.0 / N)
        return carry

    lax.fori_loop(0, GX, reduce, 0)
    over_peers(lambda k: grad_copy(k).start())
    wait_homeward()
    stores = [pltpu.make_async_copy(field.at[zz], out.at[zz], store.at[zz]) for zz in range(2)]
    for zz in range(2):
        inverse(zz)
        stores[zz].start()
    over_peers(lambda k: grad_copy(k).wait())
    gall[gx] = gsum[gx]
    total = gall[0]
    for src in range(1, GX):
        total = total + gall[src]
    grads[...] = total
    sends_done(1)
    for copy in stores:
        copy.wait()


def program(phi, coeff, goal, edge, alpha, bands):
    f32 = jnp.float32
    dma = pltpu.SemaphoreType.DMA
    tile = (ROWS, HALF)
    hbm, local = pl.BlockSpec(memory_space=pl.ANY), pl.BlockSpec(memory_space=pltpu.VMEM)
    return pl.pallas_call(
        kernel,
        out_shape=[jax.ShapeDtypeStruct((2, 4, N, N), f32), jax.ShapeDtypeStruct(tile, f32)],
        in_specs=[hbm] * 4 + [local] * (2 + TABLES),
        out_specs=[hbm, local],
        scratch_shapes=[
            pltpu.VMEM((2, 4, N, N), f32),
            pltpu.VMEM((2, N, N), f32),
            pltpu.VMEM((2, 64, 2) + tile, f32),
            pltpu.VMEM((2, 64, 4, HALF), f32),
            pltpu.VMEM((GX * SENT, HALF), f32),
            pltpu.VMEM((GX * SENT, HALF), f32),
            pltpu.VMEM((GX * BACK, HALF), f32),
            pltpu.VMEM((GX * BACK, HALF), f32),
            pltpu.VMEM((64, 12) + tile, f32),
            pltpu.VMEM((GX, 4) + tile, f32),
            pltpu.VMEM((GX, 4) + tile, f32),
            pltpu.VMEM((GX, 4) + tile, f32),
            pltpu.VMEM((2, 10) + tile, f32),
            pltpu.VMEM((2, 3, 10) + tile, f32),
            pltpu.VMEM((GX,) + tile, f32),
            pltpu.VMEM((GX,) + tile, f32),
            pltpu.VMEM((ROWS, N), f32),
            dma((5,)),
            dma((2,)),
            dma((len(OUTWARD),)),
            dma((len(HOMEWARD),)),
            dma((len(OUTWARD), GX)),
            dma((len(OUTWARD), GX)),
            dma((len(HOMEWARD), GX)),
            dma((len(HOMEWARD), GX)),
            dma((2, len(FLUXES), BA - 1)),
            dma((2, len(FLUXES), BA - 1)),
            dma((GX,)),
            dma((GX,)),
        ],
        compiler_params=pltpu.CompilerParams(collective_id=0, has_side_effects=True, vmem_limit_bytes=56 << 20),
        name="transport",
    )(phi, coeff, goal, edge, alpha, bands, *tables())


def signed(index):
    return ((index + HALF) % N - HALF).astype(jnp.float32) * BASE


def propagators(rates, speeds, gx):
    sub = jnp.arange(ROWS)[:, None]
    lane = jnp.arange(HALF)[None, :]
    rate, speed = jnp.tile(rates, 2)[:, None], jnp.tile(speeds, 2)[:, None]
    fx, fy = [], []
    for t in range(4):
        fx.append(jnp.broadcast_to(signed(gx * ROWS + 2 * t + sub // 4), (ROWS, HALF)))
        fy.append(jnp.broadcast_to(signed(lane), (ROWS, HALF)))
    kx = gx * ROWS + lane % ROWS
    line = signed(kx)
    line = jnp.where((lane >= 8) & (kx == HALF), -line, line)
    fx.append(jnp.where(sub < 4, line, HALF * BASE))
    fy.append(jnp.where(sub < 4, jnp.where(lane < 8, -HALF * BASE, HALF * BASE), signed(lane)))
    fx, fy = jnp.stack(fx)[:, None], jnp.stack(fy)[:, None]
    sx, sy = jnp.asarray(SX, jnp.float32)[None, :, None, None], jnp.asarray(SY, jnp.float32)[None, :, None, None]
    wave = speed * (sx * fx + sy * fy)
    real = rate + jnp.asarray(np.abs(COS), jnp.float32)[None, :, None, None] * speed
    denom = real * real + wave * wave
    return jnp.stack([real / denom, -wave / denom], axis=2)


def targets(forward, gx):
    low = forward[..., :HALF]
    turned = jnp.flip(jnp.roll(forward, -1, axis=4)[..., HALF:], axis=4)
    ba_free = [(i, GX - 1 - i) for i in range(GX)]
    block = lax.ppermute(jnp.flip(jnp.roll(turned, -1, axis=3), axis=3), "gx", ba_free)
    lead = lax.ppermute(turned[:, :, :, :1], "gx", [(i, (GX - i) % GX) for i in range(GX)])
    mirror = jnp.concatenate([lead, block[:, :, :, 1:]], axis=3)
    lane = jnp.arange(HALF)[None, :]
    kx = gx * ROWS + jnp.arange(ROWS)[:, None]
    mirror = jnp.where((lane > 0) & (kx != HALF), mirror, 0.0)
    sign = jnp.array([1.0, -1.0], jnp.float32).reshape(1, 2, 1, 1, 1)
    goal = jnp.swapaxes(low + sign * mirror, 1, 2)
    own = jnp.where((lane > 0) & (gx == HALF // ROWS), turned[:, :, :, 0] * sign[..., 0], 0.0)
    line = jnp.pad(forward[..., HALF], ((0, 0), (0, 0), (0, 0), (0, HALF - ROWS)))
    edge = jnp.stack([line, own], axis=3)
    edge = jnp.swapaxes(edge, 1, 2).reshape(forward.shape[0], 64, 4, HALF)
    return goal, edge


def body(phi_start, coeff, forward, rates, speeds, shares):
    gx = lax.axis_index("gx")
    goal, edge = targets(forward, gx)
    alpha = propagators(rates, speeds, gx)
    bands = jnp.broadcast_to(jnp.tile(jnp.stack([rates, speeds, shares]), (1, 2))[:, :, None], (3, ROWS, HALF))
    phi, sums = program(phi_start, coeff, goal, edge, alpha, bands)
    parts = sums[:, :24].reshape(2, 4, 2, 12)
    return (phi, jnp.transpose(parts[0] + parts[1], (1, 2, 0)))


def solution(mesh):
    in_specs = (
        P("gx", "ba", None, None),
        P("gx", None, None),
        P(None, None, None, "gx", None),
        P("ba"),
        P("ba"),
        P("ba"),
    )
    out_specs = (P("gx", "ba", None, None), P("gx", None, "ba"))
    return jax.shard_map(body, mesh=mesh, in_specs=in_specs, out_specs=out_specs, check_vma=False)
```

time: 286 us -> 192 us (0.67)
  Pallas kernels: 243 us -> 145 us
  waiting for transfers between devices: 0.01 us -> 12 us
  local copies, waits for them, and re-layouts: 23.3 us -> 18 us
    pallas_call x11 -> x1, Pallas kernels: 243 us -> 145 us  [program(): pl.pallas_call(kernel, out_shape=[jax.ShapeDtypeStruct((2, 4, N, N), f32)...]
    ppermute x1, waiting for transfers between devices: 0.01 us -> 12 us  [targets(): lax.ppermute(jnp.flip(jnp.roll(turned, -1, axis=3), axis=3), 'gx', ba_free)]
    unnamed x67 -> x32, local copies, waits for them, and re-layouts: 14.3 us -> 9.88 us
  transfers between devices with their start and end apart: 2 -> 2, of which waited for: 0 -> 1; matrix products, arithmetic and copies ran while one was open for 4% -> 7% of each run, Pallas kernels for 16% -> 0%
where the time goes in v1:
time: 192 us
  Pallas kernels  145 us (76%)
  local copies, waits for them, and re-layouts  18 us (9%)
  waiting for transfers between devices  12 us (6%)
  starting transfers between devices  9.28 us (5%)
  other arithmetic  6.79 us (4%)
    pallas_call x1, Pallas kernels, program(): pl.pallas_call(kernel, out_shape=[jax.ShapeDtypeStruct((2, 4, N, N), f32)...  145 us
    ppermute x1, waiting for transfers between devices, targets(): lax.ppermute(jnp.flip(jnp.roll(turned, -1, axis=3), axis=3), 'gx', ba_free)  12 us
    unnamed x32, local copies, waits for them, and re-layouts  9.88 us
    ppermute x1, starting transfers between devices, targets(): lax.ppermute(turned[:, :, :, :1], 'gx', [(i, (GX - i) % GX) for i in rang...  7.66 us
  transfers between devices with their start and end apart: 2, of which 1 were waited for; matrix products, arithmetic and copies ran while one was open for 7% of the time, Pallas kernels for 0%

profile of v1, /device:TPU:1, one launch (start us, length us, event | category | flops | bytes accessed | tf_op | source)
XLA Modules:
  0.0 191.5 jit_solution(14087387172219660165)
XLA Ops:
  0.6 2.3 %slice.48 = f32[2,2,64,8,255]{4,3,2,1,0:T(8,128)S(1)} slice(f32[2,2,64,8,256]{4,3,2,1,0:T(8,128)} %param.28), slice={[0:2], [0:2], [0:64], [0:8], [1:256]} | slice | bytes 4177920 | tf_op jit(solution)/shard_map/jit(_roll_static)/slice | solution.py:554
  3.0 1.1 fusion.30
  4.1 0.3 pad_maximum_fusion.4
  4.5 0.1 copy.38
  4.6 0.7 slice.51
  5.2 7.7 %collective-permute-start = (f32[2,2,64,1,128]{4,3,1,2,0:T(1,128)S(1)}, f32[2,2,64,1,128]{4,3,1,2,0:T(1,128)S(1)}, u32[]{:S(2)}, u32[]{:S(2)}) collective-permute-start(f32[2,2,64,1,128]{4,3,1,2,0:T(1,128)S(1)} %slice.51), channel_id=1, source_target_pairs={{0,0},{4,124},{8,120},{12,116},{16,112},{20,108},{24,104},{28,100}... | collective-permute-start | bytes 393224 | tf_op jit(solution)/shard_map/ppermute | solution.py:557
  12.9 0.3 pad_maximum_fusion
  13.3 0.5 slice.53
  13.9 0.2 pad_maximum_fusion.1
  14.2 1.1 rev.6
  15.3 1.6 collective-permute-start.1
  17.1 0.6 constant_dynamic-update-slice_fusion.4
  17.7 0.6 constant_dynamic-update-slice_fusion.9
  18.3 0.6 constant_dynamic-update-slice_fusion.8
  18.9 0.6 constant_dynamic-update-slice_fusion.7
  19.6 0.7 constant_dynamic-update-slice_fusion.3
  20.2 0.7 constant_dynamic-update-slice_fusion.2
  20.9 0.2 broadcast_select_fusion
  21.1 0.7 constant_dynamic-update-slice_fusion.1
  21.9 1.6 copy.36
  23.6 1.0 pad_maximum_fusion.3
  24.6 0.7 constant_dynamic-update-slice_fusion
  25.4 0.9 fusion.3
  26.4 0.8 pad_maximum_fusion.2.alpha
  27.2 12.0 %collective-permute-done.1 = f32[2,2,64,8,128]{4,3,1,2,0:T(8,128)} collective-permute-done((f32[2,2,64,8,128]{4,3,1,2,0:T(8,128)}, f32[2,2,64,8,128]{4,3,1,2,0:T(8,128)}, u32[]{:S(2)}, u32[]{:S(2)}) %collective-permute-start.1) | collective-permute-done | bytes 1048608 | tf_op jit(solution)/shard_map/ppermute | solution.py:556
  39.2 1.3 slice.58
  40.5 1.3 fusion.2.goal_in
  41.8 0.7 broadcast_in_dim.94.bands
  42.5 144.6 %transport.1 = (f32[2,4,256,256]{3,2,1,0:T(8,128)}, f32[8,128]{1,0:T(8,128)}) custom-call(f32[2,4,256,256]{3,2,1,0:T(8,128)} %phi.1, f32[2,256,256]{2,1,0:T(8,128)} %coeff_in.1, f32[2,64,2,8,128]{4,3,2,1,0:T(8,128)} %fusion.2.goal_in, f32[2,64,4,128]{3,2,1,0:T(4,128)} %bitcast.11, f32[5,12,2,8,128]{4,3,2,1,0:T(8,128)} %pad_maximum_fusion.2.alpha, ...), custom_call_target="tpu_custom_call" | custom-call | tf_op jit(solution)/shard_map/transport/pallas_call | solution.py:486
  187.0 0.8 slice_add_fusion
  187.9 0.6 copy.32
  188.5 3.0 %copy.50 = f32[2,4,256,256]{3,2,1,0:T(8,128)} copy(f32[2,4,256,256]{3,2,1,0:T(8,128)} %get-tuple-element.22) | data formatting | bytes 4194304
  (43 shorter events, 0.8 us)
Async XLA Ops:
  0.6 2.4 %copy-start = (f32[2,2,64,8,256]{4,3,2,1,0:T(8,128)S(1)}, f32[2,2,64,8,256]{4,3,2,1,0:T(8,128)}, u32[]{:S(2)}) copy-start(f32[2,2,64,8,256]{4,3,2,1,0:T(8,128)} %param.28) | copy-start | bytes 6291460
  5.2 35.3 %collective-permute-start = (f32[2,2,64,1,128]{4,3,1,2,0:T(1,128)S(1)}, f32[2,2,64,1,128]{4,3,1,2,0:T(1,128)S(1)}, u32[]{:S(2)}, u32[]{:S(2)}) collective-permute-start(f32[2,2,64,1,128]{4,3,1,2,0:T(1,128)S(1)} %slice.51), channel_id=1, source_target_pairs={{0,0},{4,124},{8,120},{12,116},{16,112},{20,108},{24,104},{28,100}... | collective-permute-start | bytes 393224 | tf_op jit(solution)/shard_map/ppermute | solution.py:557
  13.9 7.0 %copy-start.3 = (f32[2]{0:T(128)S(1)}, f32[2]{0:T(128)}, u32[]{:S(2)}) copy-start(f32[2]{0:T(128)} %constant.172.clone) | copy-start | bytes 28
  13.9 7.9 %copy-start.7 = (f32[4]{0:T(128)S(1)}, f32[4]{0:T(128)}, u32[]{:S(2)}) copy-start(f32[4]{0:T(128)} %param.29) | copy-start | bytes 52
  13.9 8.0 %copy-start.6 = (f32[4]{0:T(128)S(1)}, f32[4]{0:T(128)}, u32[]{:S(2)}) copy-start(f32[4]{0:T(128)} %param.30) | copy-start | bytes 52
  13.9 8.0 %copy-start.2 = (f32[2,2,64,8,1]{4,3,2,1,0:T(8,128)S(1)}, f32[2,2,64,8,1]{4,3,2,1,0:T(8,128)}, u32[]{:S(2)}) copy-start(f32[2,2,64,8,1]{4,3,2,1,0:T(8,128)} %get-tuple-element.8) | copy-start | bytes 24580
  14.1 11.1 %copy-start.9 = (f32[12]{0:T(128)S(1)}, f32[12]{0:T(128)}, u32[]{:S(2)}) copy-start(f32[12]{0:T(128)} %constant.175.clone) | copy-start | bytes 148
  14.1 11.2 %copy-start.4 = (f32[12]{0:T(128)S(1)}, f32[12]{0:T(128)}, u32[]{:S(2)}) copy-start(f32[12]{0:T(128)} %constant.174.clone) | copy-start | bytes 148
  14.2 11.2 %copy-start.5 = (f32[12]{0:T(128)S(1)}, f32[12]{0:T(128)}, u32[]{:S(2)}) copy-start(f32[12]{0:T(128)} %constant.173.clone) | copy-start | bytes 148
  14.2 12.1 %copy-start.8 = (f32[4]{0:T(128)S(1)}, f32[4]{0:T(128)}, u32[]{:S(2)}) copy-start(f32[4]{0:T(128)} %param.31) | copy-start | bytes 52
  15.3 23.9 %collective-permute-start.1 = (f32[2,2,64,8,128]{4,3,1,2,0:T(8,128)}, f32[2,2,64,8,128]{4,3,1,2,0:T(8,128)}, u32[]{:S(2)}, u32[]{:S(2)}) collective-permute-start(f32[2,2,64,8,128]{4,3,1,2,0:T(8,128)} %rev.6), channel_id=1, source_target_pairs={{0,124},{4,120},{8,116},{12,112},{16,108},{20,104},{24,100},{28,96... | collective-permute-start | bytes 3145736 | tf_op jit(solution)/shard_map/ppermute | solution.py:556
  23.6 16.9 %copy-start.1 = (f32[2,2,64,8,256]{4,3,2,1,0:T(8,128)S(1)}, f32[2,2,64,8,256]{4,3,2,1,0:T(8,128)}, u32[]{:S(2)}) copy-start(f32[2,2,64,8,256]{4,3,2,1,0:T(8,128)} %param.28) | copy-start | bytes 6291460

commit v2 on v1

--- a/solution.py
+++ b/solution.py
@@ -85,12 +85,12 @@
     return ref[pl.ds(pl.multiple_of(row, ROWS), ROWS), :]
 
 
-def kernel(phi, coeff_in, goal_in, edge_in, alpha, bands, *rest):
+def kernel(phi, coeff_in, target, rates, speeds, shares, *rest):
     names = [rest[2 * i : 2 * i + 2] for i in range(TABLES // 2)]
     wave_y, back_y, cos_x, sin_x, cos_rows, sin_rows, cos_cols, sin_cols = names
-    (out, grads, field, coeff, goal, edge_goal, sent, spec, made, back, acc, espec, enew, epack, flux, others,
-     gsum, gall, line_of, load, store, own, own_back, send, recv, send_back, recv_back, send_flux, recv_flux,
-     send_grad, recv_grad) = rest[TABLES:]
+    (field, grads, coeff, held, mirror, lead, lead_in, goal, edge_goal, alpha, sent, spec, made, back, acc, espec,
+     enew, epack, flux, others, gsum, gall, line_of, load, own, own_back, send, recv, send_back, recv_back, send_flux,
+     recv_flux, send_grad, recv_grad, send_turn, recv_turn, send_lead, recv_lead, send_share, recv_share) = rest[TABLES:]
     gx, ba = lax.axis_index("gx"), lax.axis_index("ba")
     barrier = pltpu.get_barrier_semaphore()
 
@@ -105,9 +105,8 @@
     loads = [
         pltpu.make_async_copy(phi.at[0], field.at[0], load.at[0]),
         pltpu.make_async_copy(phi.at[1], field.at[1], load.at[1]),
-        pltpu.make_async_copy(goal_in, goal, load.at[2]),
-        pltpu.make_async_copy(edge_in, edge_goal, load.at[3]),
-        pltpu.make_async_copy(coeff_in, coeff, load.at[4]),
+        pltpu.make_async_copy(target, held, load.at[2]),
+        pltpu.make_async_copy(coeff_in, coeff, load.at[3]),
     ]
     for copy in loads:
         copy.start()
@@ -115,7 +114,12 @@
     sub = lax.broadcasted_iota(jnp.int32, (ROWS, HALF), 0)
     lane = lax.broadcasted_iota(jnp.int32, (ROWS, HALF), 1)
     upper = sub < 4
-    rate, speed, share = bands[0], bands[1], bands[2]
+
+    def by_band(values):
+        spread = jnp.where(sub % 4 == 0, values[0], values[1])
+        return jnp.where(sub % 4 >= 2, jnp.where(sub % 4 == 2, values[2], values[3]), spread)
+
+    rate, speed, share = by_band(rates), by_band(speeds), by_band(shares)
     couple = [speed * float(abs(COS[d])) for d in range(6)]
     zero = jnp.zeros((ROWS, HALF), jnp.float32)
 
@@ -125,6 +129,121 @@
         return carry
 
     lax.fori_loop(0, 64, clear, 0)
+
+    def signed(index):
+        return (lax.rem(index + HALF, N) - HALF).astype(jnp.float32) * BASE
+
+    def propagators():
+        for t in range(5):
+            if t < 4:
+                fx, fy = signed(gx * ROWS + 2 * t + sub // 4), signed(lane)
+            else:
+                kx = gx * ROWS + lane % ROWS
+                line = signed(kx)
+                line = jnp.where((lane >= 8) & (kx == HALF), -line, line)
+                fx = jnp.where(upper, line, HALF * BASE)
+                fy = jnp.where(upper, jnp.where(lane < 8, -HALF * BASE, HALF * BASE), signed(lane))
+            for d in range(12):
+                wave = speed * (fx * float(SX[d]) + fy * float(SY[d]))
+                real = rate + speed * float(abs(COS[d]))
+                denom = real * real + wave * wave
+                alpha[t, d, 0] = real / denom
+                alpha[t, d, 1] = -wave / denom
+
+    partner, first_row = GX - 1 - gx, lax.rem(GX - gx, GX)
+    quarter = pl.ds(pl.multiple_of(ba * 16, 16), 16)
+
+    def turn_copy(s):
+        return pltpu.make_async_remote_copy(
+            src_ref=held.at[s, :, quarter, :, pl.ds(HALF, HALF)],
+            dst_ref=mirror.at[s, :, quarter],
+            send_sem=send_turn.at[s],
+            recv_sem=recv_turn.at[s],
+            device_id=(partner, ba),
+            device_id_type=MESH,
+        )
+
+    def share_copy(s, k):
+        return pltpu.make_async_remote_copy(
+            src_ref=mirror.at[s, :, quarter],
+            dst_ref=mirror.at[s, :, quarter],
+            send_sem=send_share.at[s, k - 1],
+            recv_sem=recv_share.at[s, k - 1],
+            device_id=(gx, lax.rem(ba + k, BA)),
+            device_id_type=MESH,
+        )
+
+    def lead_copy(s):
+        return pltpu.make_async_remote_copy(
+            src_ref=lead.at[s],
+            dst_ref=lead_in.at[s],
+            send_sem=send_lead.at[s],
+            recv_sem=recv_lead.at[s],
+            device_id=(first_row, ba),
+            device_id_type=MESH,
+        )
+
+    def lead_rows(s):
+        for c in range(2):
+            def one(z, carry):
+                lead[s, c, pl.ds(z, 1), :] = held[s, c, z, 0:1, HALF:]
+                return carry
+
+            lax.fori_loop(0, 64, one, 0)
+
+    def start_turn(s):
+        turn_copy(s).start()
+
+        @pl.when(first_row != gx)
+        def _():
+            lead_copy(s).start()
+
+    def start_share(s):
+        turn_copy(s).wait_recv()
+        for k in range(1, BA):
+            share_copy(s, k).start()
+
+    def fold(s):
+        for k in range(1, BA):
+            share_copy(s, k).wait_recv()
+
+        @pl.when(first_row != gx)
+        def _():
+            lead_copy(s).wait_recv()
+
+        @pl.when(first_row == gx)
+        def _():
+            lead_in[s] = lead[s]
+
+        lanes = lax.rem(HALF - lane, HALF)
+        rows = lax.rem(ROWS - sub, ROWS)
+        keep = (lane > 0) & ((gx != HALF // ROWS) | (sub > 0))
+        alone = (lane > 0) & (gx == HALF // ROWS)
+
+        def cell(z, carry):
+            for c in range(2):
+                tile = jnp.where(sub == 0, lead_in[s, c, pl.ds(z, 1), :], mirror[s, c, z])
+                tile = jnp.take_along_axis(jnp.take_along_axis(tile, lanes, axis=1), rows, axis=0)
+                tile = jnp.where(keep, tile, 0.0)
+                low, high = held[s, c, z, :, :HALF], held[s, c, z, :, HALF:]
+                goal[z, c] = low + tile if c == 0 else low - tile
+                line = jnp.sum(jnp.where(lane == sub, jnp.broadcast_to(high[:, 0:1], (ROWS, HALF)), 0.0), axis=0, keepdims=True)
+                other = jnp.where(alone, jnp.take_along_axis(high, lanes, axis=1), 0.0)
+                other = other[0:1] if c == 0 else -other[0:1]
+                edge_goal[z, c] = jnp.where(upper, line, other)
+            return carry
+
+        lax.fori_loop(0, 64, cell, 0)
+
+    def turns_done():
+        for s in range(2):
+            turn_copy(s).wait_send()
+            for k in range(1, BA):
+                share_copy(s, k).wait_send()
+
+            @pl.when(first_row != gx)
+            def _():
+                lead_copy(s).wait_send()
 
     def outward(message, k):
         first, count = OUTWARD[message]
@@ -259,7 +378,7 @@
             tile = jnp.where((lane >= 72) & (lane < 80), pltpu.roll(im, (HALF + 72 - off) % HALF, 1), tile)
             sent[m * SENT + 32 : m * SENT + 40, :] = tile
 
-    def inverse(zz):
+    def inverse(zz, last):
         def plane(b, carry):
             parts = []
             for part in range(2):
@@ -274,7 +393,8 @@
             u = product(both(cos_cols), modes)
             v = product(both(sin_cols), modes)
             rows = jnp.concatenate([u[:, :HALF] - v[:, HALF:], u[:, HALF:] + v[:, :HALF]], axis=1)
-            field[zz, b] = product(split(rows), both(back_y)) * coeff[zz]
+            value = product(split(rows), both(back_y))
+            field[zz, b] = value if last else value * coeff[zz]
             return carry
 
         lax.fori_loop(0, 4, plane, 0)
@@ -308,15 +428,12 @@
                 z = 2 * src + zz
                 if edge:
                     s_re, s_im = espec[src, zz], espec[src, 2 + zz]
-                    g = [
-                        jnp.where(upper, edge_goal[s, z, 2 * c : 2 * c + 1], edge_goal[s, z, 2 * c + 1 : 2 * c + 2])
-                        for c in range(2)
-                    ]
+                    g = [edge_goal[z, c] for c in range(2)]
                 else:
                     s_re = tile_of(spec, src * SENT + spot(t, zz, 0) * ROWS)
                     s_im = tile_of(spec, src * SENT + spot(t, zz, 1) * ROWS)
                     g = [
-                        jnp.where(upper, goal[s, z, c, 2 * t : 2 * t + 1], goal[s, z, c, 2 * t + 1 : 2 * t + 2])
+                        jnp.where(upper, goal[z, c, 2 * t : 2 * t + 1], goal[z, c, 2 * t + 1 : 2 * t + 2])
                         for c in range(2)
                     ]
                 s_re, s_im = s_re * rate, s_im * rate
@@ -392,7 +509,7 @@
         def _():
             wait_homeward()
             sends_done(s - 1)
-            inverse(0)
+            inverse(0, False)
 
         @pl.when(s == 0)
         def _():
@@ -402,13 +519,17 @@
 
         @pl.when(s == 0)
         def _():
+            loads[2].wait()
+            lead_rows(0)
+            lead_rows(1)
             pl.semaphore_wait(barrier, GX - 1 + BA - 1)
+            start_turn(0)
 
         start_outward(0)
 
         @pl.when(s > 0)
         def _():
-            inverse(1)
+            inverse(1, False)
 
         @pl.when(s == 0)
         def _():
@@ -421,8 +542,16 @@
 
         @pl.when(s == 0)
         def _():
-            for copy in loads[2:]:
-                copy.wait()
+            start_turn(1)
+            start_share(0)
+            propagators()
+            loads[3].wait()
+
+        fold(s)
+
+        @pl.when(s == 0)
+        def _():
+            start_share(1)
 
         wait_outward(0)
         wait_outward(1)
@@ -463,10 +592,8 @@
     lax.fori_loop(0, GX, reduce, 0)
     over_peers(lambda k: grad_copy(k).start())
     wait_homeward()
-    stores = [pltpu.make_async_copy(field.at[zz], out.at[zz], store.at[zz]) for zz in range(2)]
     for zz in range(2):
-        inverse(zz)
-        stores[zz].start()
+        inverse(zz, True)
     over_peers(lambda k: grad_copy(k).wait())
     gall[gx] = gsum[gx]
     total = gall[0]
@@ -474,11 +601,10 @@
         total = total + gall[src]
     grads[...] = total
     sends_done(1)
-    for copy in stores:
-        copy.wait()
-
-
-def program(phi, coeff, goal, edge, alpha, bands):
+    turns_done()
+
+
+def program(phi, coeff, target, rates, speeds, shares):
     f32 = jnp.float32
     dma = pltpu.SemaphoreType.DMA
     tile = (ROWS, HALF)
@@ -486,13 +612,17 @@
     return pl.pallas_call(
         kernel,
         out_shape=[jax.ShapeDtypeStruct((2, 4, N, N), f32), jax.ShapeDtypeStruct(tile, f32)],
-        in_specs=[hbm] * 4 + [local] * (2 + TABLES),
-        out_specs=[hbm, local],
+        in_specs=[hbm] * 3 + [pl.BlockSpec(memory_space=pltpu.SMEM)] * 3 + [local] * TABLES,
+        out_specs=[local, local],
         scratch_shapes=[
-            pltpu.VMEM((2, 4, N, N), f32),
             pltpu.VMEM((2, N, N), f32),
-            pltpu.VMEM((2, 64, 2) + tile, f32),
-            pltpu.VMEM((2, 64, 4, HALF), f32),
+            pltpu.VMEM((2, 2, 64, ROWS, N), f32),
+            pltpu.VMEM((2, 2, 64) + tile, f32),
+            pltpu.VMEM((2, 2, 64, HALF), f32),
+            pltpu.VMEM((2, 2, 64, HALF), f32),
+            pltpu.VMEM((64, 2) + tile, f32),
+            pltpu.VMEM((64, 2) + tile, f32),
+            pltpu.VMEM((5, 12, 2) + tile, f32),
             pltpu.VMEM((GX * SENT, HALF), f32),
             pltpu.VMEM((GX * SENT, HALF), f32),
             pltpu.VMEM((GX * BACK, HALF), f32),
@@ -506,8 +636,7 @@
             pltpu.VMEM((GX,) + tile, f32),
             pltpu.VMEM((GX,) + tile, f32),
             pltpu.VMEM((ROWS, N), f32),
-            dma((5,)),
-            dma((2,)),
+            dma((4,)),
             dma((len(OUTWARD),)),
             dma((len(HOMEWARD),)),
             dma((len(OUTWARD), GX)),
@@ -518,62 +647,21 @@
             dma((2, len(FLUXES), BA - 1)),
             dma((GX,)),
             dma((GX,)),
+            dma((2,)),
+            dma((2,)),
+            dma((2,)),
+            dma((2,)),
+            dma((2, BA - 1)),
+            dma((2, BA - 1)),
         ],
         compiler_params=pltpu.CompilerParams(collective_id=0, has_side_effects=True, vmem_limit_bytes=56 << 20),
         name="transport",
-    )(phi, coeff, goal, edge, alpha, bands, *tables())
-
-
-def signed(index):
-    return ((index + HALF) % N - HALF).astype(jnp.float32) * BASE
-
-
-def propagators(rates, speeds, gx):
-    sub = jnp.arange(ROWS)[:, None]
-    lane = jnp.arange(HALF)[None, :]
-    rate, speed = jnp.tile(rates, 2)[:, None], jnp.tile(speeds, 2)[:, None]
-    fx, fy = [], []
-    for t in range(4):
-        fx.append(jnp.broadcast_to(signed(gx * ROWS + 2 * t + sub // 4), (ROWS, HALF)))
-        fy.append(jnp.broadcast_to(signed(lane), (ROWS, HALF)))
-    kx = gx * ROWS + lane % ROWS
-    line = signed(kx)
-    line = jnp.where((lane >= 8) & (kx == HALF), -line, line)
-    fx.append(jnp.where(sub < 4, line, HALF * BASE))
-    fy.append(jnp.where(sub < 4, jnp.where(lane < 8, -HALF * BASE, HALF * BASE), signed(lane)))
-    fx, fy = jnp.stack(fx)[:, None], jnp.stack(fy)[:, None]
-    sx, sy = jnp.asarray(SX, jnp.float32)[None, :, None, None], jnp.asarray(SY, jnp.float32)[None, :, None, None]
-    wave = speed * (sx * fx + sy * fy)
-    real = rate + jnp.asarray(np.abs(COS), jnp.float32)[None, :, None, None] * speed
-    denom = real * real + wave * wave
-    return jnp.stack([real / denom, -wave / denom], axis=2)
-
-
-def targets(forward, gx):
-    low = forward[..., :HALF]
-    turned = jnp.flip(jnp.roll(forward, -1, axis=4)[..., HALF:], axis=4)
-    ba_free = [(i, GX - 1 - i) for i in range(GX)]
-    block = lax.ppermute(jnp.flip(jnp.roll(turned, -1, axis=3), axis=3), "gx", ba_free)
-    lead = lax.ppermute(turned[:, :, :, :1], "gx", [(i, (GX - i) % GX) for i in range(GX)])
-    mirror = jnp.concatenate([lead, block[:, :, :, 1:]], axis=3)
-    lane = jnp.arange(HALF)[None, :]
-    kx = gx * ROWS + jnp.arange(ROWS)[:, None]
-    mirror = jnp.where((lane > 0) & (kx != HALF), mirror, 0.0)
-    sign = jnp.array([1.0, -1.0], jnp.float32).reshape(1, 2, 1, 1, 1)
-    goal = jnp.swapaxes(low + sign * mirror, 1, 2)
-    own = jnp.where((lane > 0) & (gx == HALF // ROWS), turned[:, :, :, 0] * sign[..., 0], 0.0)
-    line = jnp.pad(forward[..., HALF], ((0, 0), (0, 0), (0, 0), (0, HALF - ROWS)))
-    edge = jnp.stack([line, own], axis=3)
-    edge = jnp.swapaxes(edge, 1, 2).reshape(forward.shape[0], 64, 4, HALF)
-    return goal, edge
+    )(phi, coeff, target, rates, speeds, shares, *tables())
 
 
 def body(phi_start, coeff, forward, rates, speeds, shares):
-    gx = lax.axis_index("gx")
-    goal, edge = targets(forward, gx)
-    alpha = propagators(rates, speeds, gx)
-    bands = jnp.broadcast_to(jnp.tile(jnp.stack([rates, speeds, shares]), (1, 2))[:, :, None], (3, ROWS, HALF))
-    phi, sums = program(phi_start, coeff, goal, edge, alpha, bands)
+    phi, sums = program(phi_start, coeff, forward, rates, speeds, shares)
+    phi = phi * coeff[:, None]
     parts = sums[:, :24].reshape(2, 4, 2, 12)
     return (phi, jnp.transpose(parts[0] + parts[1], (1, 2, 0)))
 

time: 192 us -> 174 us (0.906)
  Pallas kernels: 145 us -> 169 us
  local copies, waits for them, and re-layouts: 18 us -> 0.69 us
  waiting for transfers between devices: 12 us -> 0 us
  starting transfers between devices: 9.28 us -> 0 us
  other arithmetic: 6.79 us -> 3.11 us
    pallas_call x1, Pallas kernels: 145 us -> 169 us  [program(): pl.pallas_call(kernel, out_shape=[jax.ShapeDtypeStruct((2, 4, N, N), f32)...]
    ppermute x2 -> x0, waiting for transfers between devices: 12 us -> none  [the longest x1 12 us: targets(): lax.ppermute(jnp.flip(jnp.roll(turned, -1, axis=3), axis=3), 'gx', ba_free)]
    ppermute x2 -> x0, starting transfers between devices: 9.28 us -> none  [the longest x1 7.66 us: targets(): lax.ppermute(turned[:, :, :, :1], 'gx', [(i, (GX - i) % GX) for i in rang...]
    unnamed x32 -> x5, local copies, waits for them, and re-layouts: 9.88 us -> 0.61 us
    slice x5 -> x0, local copies, waits for them, and re-layouts: 5.97 us -> none  [the longest x1 2.34 us: targets(): turned = jnp.flip(jnp.roll(forward, -1, axis=4)[..., HALF:], axis=4)]
    mul x5 -> x1, other arithmetic: 0.08 us -> 3.1 us  [body(): phi = phi * coeff[:, None]]
    another operation x4 -> x0, other arithmetic: 2.49 us -> none  [the longest x1 0.97 us: targets(): edge = jnp.stack([line, own], axis=3)]
  transfers between devices with their start and end apart: 2 -> 0, of which waited for: 1 -> 0; matrix products, arithmetic and copies ran while one was open for 7% -> 0% of each run, Pallas kernels for 0% -> 0%
where the time goes in v2:
time: 174 us
  Pallas kernels  169 us (97%)
  other arithmetic  3.11 us (2%)
    pallas_call x1, Pallas kernels, program(): pl.pallas_call(kernel, out_shape=[jax.ShapeDtypeStruct((2, 4, N, N), f32)...  169 us

profile of v2, /device:TPU:1, one launch (start us, length us, event | category | flops | bytes accessed | tf_op | source)
XLA Modules:
  0.0 173.6 jit_solution(14425920745049367213)
XLA Ops:
  0.6 0.0 copy-start
  0.6 169.1 %transport.1 = (f32[2,4,256,256]{3,2,1,0:T(8,128)}, f32[8,128]{1,0:T(8,128)}) custom-call(f32[2,4,256,256]{3,2,1,0:T(8,128)} %phi.1, f32[2,256,256]{2,1,0:T(8,128)} %coeff_in.1, f32[2,2,64,8,256]{4,3,2,1,0:T(8,128)} %target.1, f32[4]{0:T(128)} %rates.1, f32[4]{0:T(128)} %speeds.1, f32[4]{0:T(128)} %shares.1, bf16[256,256]{1,0:T(8,128)(2,1)} %constant.32.clone.rest_0_, ...), custom_call_target="tpu_custom_call" | custom-call | tf_op jit(solution)/shard_map/transport/pallas_call | solution.py:612
  169.7 0.0 copy-done
  169.8 0.0 copy-start.1
  169.8 3.1 %broadcast_multiply_fusion = f32[2,4,256,256]{3,2,1,0:T(8,128)} fusion(f32[2,4,256,256]{3,2,1,0:T(8,128)} %get-tuple-element.4, f32[2,256,256]{2,1,0:T(8,128)S(1)} %copy-done), kind=kLoop, calls=%fused_computation | loop fusion | flops 524288 | bytes 4718592 | tf_op jit(solution)/shard_map/mul | solution.py:664
  172.9 0.0 copy-done.1
  172.9 0.1 add.7
  173.0 0.6 copy.24
  (1 shorter events, 0.0 us)
Async XLA Ops:
  0.6 169.1 %copy-start = (f32[2,256,256]{2,1,0:T(8,128)S(1)}, f32[2,256,256]{2,1,0:T(8,128)}, u32[]{:S(2)}) copy-start(f32[2,256,256]{2,1,0:T(8,128)} %coeff_in.1) | copy-start | bytes 1572868
  169.8 3.1 %copy-start.1 = (f32[8,128]{1,0:T(8,128)S(1)}, f32[8,128]{1,0:T(8,128)}, u32[]{:S(2)}) copy-start(f32[8,128]{1,0:T(8,128)} %get-tuple-element.5) | copy-start | bytes 12292

commit v3 on v2

--- a/solution.py
+++ b/solution.py
@@ -185,11 +185,7 @@
 
     def lead_rows(s):
         for c in range(2):
-            def one(z, carry):
-                lead[s, c, pl.ds(z, 1), :] = held[s, c, z, 0:1, HALF:]
-                return carry
-
-            lax.fori_loop(0, 64, one, 0)
+            lead[s, c] = held[s, c, :, 0, HALF:]
 
     def start_turn(s):
         turn_copy(s).start()
@@ -220,8 +216,8 @@
         keep = (lane > 0) & ((gx != HALF // ROWS) | (sub > 0))
         alone = (lane > 0) & (gx == HALF // ROWS)
 
-        def cell(z, carry):
-            for c in range(2):
+        def cell(block, carry):
+            for z, c in [(8 * block + i, c) for i in range(8) for c in range(2)]:
                 tile = jnp.where(sub == 0, lead_in[s, c, pl.ds(z, 1), :], mirror[s, c, z])
                 tile = jnp.take_along_axis(jnp.take_along_axis(tile, lanes, axis=1), rows, axis=0)
                 tile = jnp.where(keep, tile, 0.0)
@@ -233,7 +229,7 @@
                 edge_goal[z, c] = jnp.where(upper, line, other)
             return carry
 
-        lax.fori_loop(0, 64, cell, 0)
+        lax.fori_loop(0, 8, cell, 0)
 
     def turns_done():
         for s in range(2):
@@ -400,10 +396,10 @@
         lax.fori_loop(0, 4, plane, 0)
 
     def gather():
-        def one(src, carry):
-            base = src * SENT
-            line = tile_of(spec, base + 4 * ROWS)
-            for zz in range(2):
+        def one(block, carry):
+            for src, zz in [(4 * block + i, zz) for i in range(4) for zz in range(2)]:
+                base = src * SENT
+                line = tile_of(spec, base + 4 * ROWS)
                 col = line if zz == 0 else pltpu.roll(line, 4, 0)
                 col_re = jnp.where(lane < 16, col, 0.0)
                 col_im = jnp.where(lane < 16, pltpu.roll(col, 64, 1), 0.0)
@@ -413,7 +409,7 @@
                 )
             return carry
 
-        lax.fori_loop(0, GX, one, 0)
+        lax.fori_loop(0, GX // 4, one, 0)
 
     mean = jnp.where(upper & (gx == HALF // ROWS), 0.5, 0.0)
 
@@ -502,6 +498,14 @@
         for k in range(1, BA):
             wall_copy(s, message, k).wait_recv()
 
+    propagators()
+    loads[2].wait()
+    for s in range(2):
+        lead_rows(s)
+    pl.semaphore_wait(barrier, GX - 1 + BA - 1)
+    for s in range(2):
+        start_turn(s)
+
     def one_step(s, carry):
         line_of[...] = jnp.zeros_like(line_of)
 
@@ -516,52 +520,39 @@
             loads[0].wait()
 
         forward(0)
+        start_outward(0)
+
+        @pl.when(s > 0)
+        def _():
+            inverse(1, False)
 
         @pl.when(s == 0)
         def _():
-            loads[2].wait()
-            lead_rows(0)
-            lead_rows(1)
-            pl.semaphore_wait(barrier, GX - 1 + BA - 1)
-            start_turn(0)
-
-        start_outward(0)
-
-        @pl.when(s > 0)
-        def _():
-            inverse(1, False)
-
-        @pl.when(s == 0)
-        def _():
-            loads[1].wait()
+            for copy in (loads[1], loads[3]):
+                copy.wait()
 
         forward(1)
         edges()
-        for message in range(1, len(OUTWARD)):
-            start_outward(message)
 
         @pl.when(s == 0)
         def _():
-            start_turn(1)
             start_share(0)
-            propagators()
-            loads[3].wait()
-
+            start_share(1)
+
+        start_outward(1)
+        start_outward(2)
         fold(s)
-
-        @pl.when(s == 0)
-        def _():
-            start_share(1)
-
         wait_outward(0)
         wait_outward(1)
         gather()
         down(s, 4)
         down(s, 0)
         start_wall(s, 0)
+        start_outward(3)
         wait_outward(2)
         down(s, 1)
         start_wall(s, 1)
+        start_outward(4)
         wait_wall(s, 0)
         up(s, 4)
         up(s, 0)

time: 174 us -> 156 us (0.90)
  Pallas kernels: 169 us -> 151 us
    pallas_call x1, Pallas kernels: 169 us -> 151 us  [program(): pl.pallas_call(kernel, out_shape=[jax.ShapeDtypeStruct((2, 4, N, N), f32)...]
where the time goes in v3:
time: 156 us
  Pallas kernels  151 us (97%)
  other arithmetic  3.11 us (2%)
    pallas_call x1, Pallas kernels, program(): pl.pallas_call(kernel, out_shape=[jax.ShapeDtypeStruct((2, 4, N, N), f32)...  151 us

profile of v3, /device:TPU:1, one launch (start us, length us, event | category | flops | bytes accessed | tf_op | source)
XLA Modules:
  0.0 155.8 jit_solution(3116955546816245007)
XLA Ops:
  0.6 0.0 copy-start
  0.6 151.3 %transport.1 = (f32[2,4,256,256]{3,2,1,0:T(8,128)}, f32[8,128]{1,0:T(8,128)}) custom-call(f32[2,4,256,256]{3,2,1,0:T(8,128)} %phi.1, f32[2,256,256]{2,1,0:T(8,128)} %coeff_in.1, f32[2,2,64,8,256]{4,3,2,1,0:T(8,128)} %target.1, f32[4]{0:T(128)} %rates.1, f32[4]{0:T(128)} %speeds.1, f32[4]{0:T(128)} %shares.1, bf16[256,256]{1,0:T(8,128)(2,1)} %constant.32.clone.rest_0_, ...), custom_call_target="tpu_custom_call" | custom-call | tf_op jit(solution)/shard_map/transport/pallas_call | solution.py:603
  152.0 0.0 copy-done
  152.0 0.0 copy-start.1
  152.0 3.1 %broadcast_multiply_fusion = f32[2,4,256,256]{3,2,1,0:T(8,128)} fusion(f32[2,4,256,256]{3,2,1,0:T(8,128)} %get-tuple-element.4, f32[2,256,256]{2,1,0:T(8,128)S(1)} %copy-done), kind=kLoop, calls=%fused_computation | loop fusion | flops 524288 | bytes 4718592 | tf_op jit(solution)/shard_map/mul | solution.py:655
  155.1 0.0 copy-done.1
  155.1 0.1 add.7
  155.2 0.6 copy.24
  (1 shorter events, 0.0 us)
Async XLA Ops:
  0.6 151.3 %copy-start = (f32[2,256,256]{2,1,0:T(8,128)S(1)}, f32[2,256,256]{2,1,0:T(8,128)}, u32[]{:S(2)}) copy-start(f32[2,256,256]{2,1,0:T(8,128)} %coeff_in.1) | copy-start | bytes 1572868
  152.0 3.1 %copy-start.1 = (f32[8,128]{1,0:T(8,128)S(1)}, f32[8,128]{1,0:T(8,128)}, u32[]{:S(2)}) copy-start(f32[8,128]{1,0:T(8,128)} %get-tuple-element.5) | copy-start | bytes 12292

commit v4 on v3

--- a/solution.py
+++ b/solution.py
@@ -338,28 +338,32 @@
         return pair[0][...], pair[1][...]
 
     def forward(zz):
-        def plane(b, carry):
-            value = split(field[zz, b])
-            rows = split(product(value, both(wave_y)))
-            u = product(both(cos_rows), rows)
-            v = product(both(sin_rows), rows)
-            re = u[:, :HALF] + jnp.where(inner, v[:, HALF:], 0.0)
-            im = jnp.where(inner, u[:, HALF:], 0.0) - v[:, :HALF]
-            for t in range(4):
-                for r in range(2):
-                    for m in range(0, GX, ROWS):
-                        at = (2 * t + r) * GX + m
-                        for part, value_ in ((0, re), (1, im)):
-                            row = m * SENT + spot(t, zz, part) * ROWS + r * 4
-                            sent[pl.ds(row + b, ROWS, stride=SENT), :] = value_[at : at + ROWS]
-            pick = jnp.where(row8 == zz * 4 + b, sign, 0.0).astype(jnp.bfloat16)
+        def planes(pair, carry):
+            both_b = (2 * pair, 2 * pair + 1)
+            values = [split(field[zz, b]) for b in both_b]
+            rows = [split(product(value, both(wave_y))) for value in values]
+            us = [product(both(cos_rows), row) for row in rows]
+            vs = [product(both(sin_rows), row) for row in rows]
+            for b, u, v in zip(both_b, us, vs):
+                re = u[:, :HALF] + jnp.where(inner, v[:, HALF:], 0.0)
+                im = jnp.where(inner, u[:, HALF:], 0.0) - v[:, :HALF]
+                for t in range(4):
+                    for r in range(2):
+                        for m in range(0, GX, ROWS):
+                            at = (2 * t + r) * GX + m
+                            for part, value in ((0, re), (1, im)):
+                                row = m * SENT + spot(t, zz, part) * ROWS + r * 4
+                                sent[pl.ds(row + b, ROWS, stride=SENT), :] = value[at : at + ROWS]
             nt = (((1,), (1,)), ((), ()))
-            line_of[...] += lax.dot_general(
-                pick, value[0], nt, preferred_element_type=jnp.float32
-            ) + lax.dot_general(pick, value[1], nt, preferred_element_type=jnp.float32)
+            total = line_of[...]
+            for b, value in zip(both_b, values):
+                pick = jnp.where(row8 == zz * 4 + b, sign, 0.0).astype(jnp.bfloat16)
+                for half in value:
+                    total += lax.dot_general(pick, half, nt, preferred_element_type=jnp.float32)
+            line_of[...] = total
             return carry
 
-        lax.fori_loop(0, 4, plane, 0)
+        lax.fori_loop(0, 2, planes, 0)
 
     def edges():
         line = split(line_of[...])
@@ -375,7 +379,7 @@
             sent[m * SENT + 32 : m * SENT + 40, :] = tile
 
     def inverse(zz, last):
-        def plane(b, carry):
+        def modes_of(b):
             parts = []
             for part in range(2):
                 pieces = []
@@ -385,15 +389,23 @@
                             row = m * BACK + (4 * t + 2 * zz + part) * ROWS + r * 4
                             pieces.append(back[pl.ds(row + b, ROWS, stride=BACK), :])
                 parts.append(jnp.concatenate(pieces, axis=0))
-            modes = split(jnp.concatenate(parts, axis=1))
-            u = product(both(cos_cols), modes)
-            v = product(both(sin_cols), modes)
-            rows = jnp.concatenate([u[:, :HALF] - v[:, HALF:], u[:, HALF:] + v[:, :HALF]], axis=1)
-            value = product(split(rows), both(back_y))
-            field[zz, b] = value if last else value * coeff[zz]
+            return split(jnp.concatenate(parts, axis=1))
+
+        def planes(pair, carry):
+            both_b = (2 * pair, 2 * pair + 1)
+            modes = [modes_of(b) for b in both_b]
+            us = [product(both(cos_cols), mode) for mode in modes]
+            vs = [product(both(sin_cols), mode) for mode in modes]
+            rows = [
+                split(jnp.concatenate([u[:, :HALF] - v[:, HALF:], u[:, HALF:] + v[:, :HALF]], axis=1))
+                for u, v in zip(us, vs)
+            ]
+            for b, row in zip(both_b, rows):
+                value = product(row, both(back_y))
+                field[zz, b] = value if last else value * coeff[zz]
             return carry
 
-        lax.fori_loop(0, 4, plane, 0)
+        lax.fori_loop(0, 2, planes, 0)
 
     def gather():
         def one(block, carry):

time: 156 us -> 150 us (0.962)
  Pallas kernels: 151 us -> 145 us
    pallas_call x1, Pallas kernels: 151 us -> 145 us  [program(): pl.pallas_call(kernel, out_shape=[jax.ShapeDtypeStruct((2, 4, N, N), f32)...]
where the time goes in v4:
time: 150 us; the launch traced here: 149 us
  Pallas kernels  145 us (97%)
  other arithmetic  3.11 us (2%)
    pallas_call x1, Pallas kernels, program(): pl.pallas_call(kernel, out_shape=[jax.ShapeDtypeStruct((2, 4, N, N), f32)...  145 us
    mul x1, other arithmetic, body(): phi = phi * coeff[:, None]  3.1 us

profile of v4, /device:TPU:1, one launch (start us, length us, event | category | flops | bytes accessed | tf_op | source)
XLA Modules:
  0.0 149.5 jit_solution(4795116038237774572)
XLA Ops:
  0.6 0.0 copy-start
  0.6 145.0 %transport.1 = (f32[2,4,256,256]{3,2,1,0:T(8,128)}, f32[8,128]{1,0:T(8,128)}) custom-call(f32[2,4,256,256]{3,2,1,0:T(8,128)} %phi.1, f32[2,256,256]{2,1,0:T(8,128)} %coeff_in.1, f32[2,2,64,8,256]{4,3,2,1,0:T(8,128)} %target.1, f32[4]{0:T(128)} %rates.1, f32[4]{0:T(128)} %speeds.1, f32[4]{0:T(128)} %shares.1, bf16[256,256]{1,0:T(8,128)(2,1)} %constant.32.clone.rest_0_, ...), custom_call_target="tpu_custom_call" | custom-call | tf_op jit(solution)/shard_map/transport/pallas_call | solution.py:615
  145.6 0.0 copy-done
  145.7 0.0 copy-start.1
  145.7 3.1 %broadcast_multiply_fusion = f32[2,4,256,256]{3,2,1,0:T(8,128)} fusion(f32[2,4,256,256]{3,2,1,0:T(8,128)} %get-tuple-element.4, f32[2,256,256]{2,1,0:T(8,128)S(1)} %copy-done), kind=kLoop, calls=%fused_computation | loop fusion | flops 524288 | bytes 4718592 | tf_op jit(solution)/shard_map/mul | solution.py:667
  148.8 0.0 copy-done.1
  148.8 0.1 add.7
  148.9 0.6 copy.24
  (1 shorter events, 0.0 us)
Async XLA Ops:
  0.6 145.0 %copy-start = (f32[2,256,256]{2,1,0:T(8,128)S(1)}, f32[2,256,256]{2,1,0:T(8,128)}, u32[]{:S(2)}) copy-start(f32[2,256,256]{2,1,0:T(8,128)} %coeff_in.1) | copy-start | bytes 1572868
  145.7 3.1 %copy-start.1 = (f32[8,128]{1,0:T(8,128)S(1)}, f32[8,128]{1,0:T(8,128)}, u32[]{:S(2)}) copy-start(f32[8,128]{1,0:T(8,128)} %get-tuple-element.5) | copy-start | bytes 12292

commit v5 on v4

--- a/solution.py
+++ b/solution.py
@@ -67,6 +67,15 @@
     rh, rl = right
     dot = functools.partial(jnp.dot, preferred_element_type=jnp.float32)
     return dot(lh, rh) + (dot(ll, rh) + dot(lh, rl))
+
+
+def stacked(lefts, right):
+    dot = functools.partial(jnp.dot, preferred_element_type=jnp.float32)
+    count = len(lefts)
+    first = dot(jnp.concatenate([left[0] for left in lefts] + [left[1] for left in lefts], axis=0), right[0])
+    second = dot(jnp.concatenate([left[0] for left in lefts], axis=0), right[1])
+    cut = [slice(N * i, N * (i + 1)) for i in range(2 * count)]
+    return [first[cut[i]] + (first[cut[count + i]] + second[cut[i]]) for i in range(count)]
 
 
 SENT = 136
@@ -341,10 +350,9 @@
         def planes(pair, carry):
             both_b = (2 * pair, 2 * pair + 1)
             values = [split(field[zz, b]) for b in both_b]
-            rows = [split(product(value, both(wave_y))) for value in values]
-            us = [product(both(cos_rows), row) for row in rows]
-            vs = [product(both(sin_rows), row) for row in rows]
-            for b, u, v in zip(both_b, us, vs):
+            rows = [split(value) for value in stacked(values, both(wave_y))]
+            uvs = [stacked((both(cos_rows), both(sin_rows)), row) for row in rows]
+            for b, (u, v) in zip(both_b, uvs):
                 re = u[:, :HALF] + jnp.where(inner, v[:, HALF:], 0.0)
                 im = jnp.where(inner, u[:, HALF:], 0.0) - v[:, :HALF]
                 for t in range(4):
@@ -394,14 +402,12 @@
         def planes(pair, carry):
             both_b = (2 * pair, 2 * pair + 1)
             modes = [modes_of(b) for b in both_b]
-            us = [product(both(cos_cols), mode) for mode in modes]
-            vs = [product(both(sin_cols), mode) for mode in modes]
+            uvs = [stacked((both(cos_cols), both(sin_cols)), mode) for mode in modes]
             rows = [
                 split(jnp.concatenate([u[:, :HALF] - v[:, HALF:], u[:, HALF:] + v[:, :HALF]], axis=1))
-                for u, v in zip(us, vs)
+                for u, v in uvs
             ]
-            for b, row in zip(both_b, rows):
-                value = product(row, both(back_y))
+            for b, value in zip(both_b, [product(row, both(back_y)) for row in rows]):
                 field[zz, b] = value if last else value * coeff[zz]
             return carry
 

time: 150 us -> 150 us (level)
  no operation moved by 1% of the time
where the time goes in v5:
time: 150 us
  Pallas kernels  145 us (97%)
  other arithmetic  3.11 us (2%)
    pallas_call x1, Pallas kernels, program(): pl.pallas_call(kernel, out_shape=[jax.ShapeDtypeStruct((2, 4, N, N), f32)...  145 us
    mul x1, other arithmetic, body(): phi = phi * coeff[:, None]  3.1 us

profile of v5, /device:TPU:1, one launch (start us, length us, event | category | flops | bytes accessed | tf_op | source)
XLA Modules:
  0.0 149.9 jit_solution(5996126771922924736)
XLA Ops:
  0.6 0.0 copy-start
  0.6 145.4 %transport.1 = (f32[2,4,256,256]{3,2,1,0:T(8,128)}, f32[8,128]{1,0:T(8,128)}) custom-call(f32[2,4,256,256]{3,2,1,0:T(8,128)} %phi.1, f32[2,256,256]{2,1,0:T(8,128)} %coeff_in.1, f32[2,2,64,8,256]{4,3,2,1,0:T(8,128)} %target.1, f32[4]{0:T(128)} %rates.1, f32[4]{0:T(128)} %speeds.1, f32[4]{0:T(128)} %shares.1, bf16[256,256]{1,0:T(8,128)(2,1)} %constant.32.clone.rest_0_, ...), custom_call_target="tpu_custom_call" | custom-call | tf_op jit(solution)/shard_map/transport/pallas_call | solution.py:621
  146.1 0.0 copy-done
  146.1 0.0 copy-start.1
  146.1 3.1 %broadcast_multiply_fusion = f32[2,4,256,256]{3,2,1,0:T(8,128)} fusion(f32[2,4,256,256]{3,2,1,0:T(8,128)} %get-tuple-element.4, f32[2,256,256]{2,1,0:T(8,128)S(1)} %copy-done), kind=kLoop, calls=%fused_computation | loop fusion | flops 524288 | bytes 4718592 | tf_op jit(solution)/shard_map/mul | solution.py:673
  149.2 0.0 copy-done.1
  149.2 0.1 add.7
  149.3 0.6 copy.24
  (1 shorter events, 0.0 us)
Async XLA Ops:
  0.6 145.5 %copy-start = (f32[2,256,256]{2,1,0:T(8,128)S(1)}, f32[2,256,256]{2,1,0:T(8,128)}, u32[]{:S(2)}) copy-start(f32[2,256,256]{2,1,0:T(8,128)} %coeff_in.1) | copy-start | bytes 1572868
  146.1 3.1 %copy-start.1 = (f32[8,128]{1,0:T(8,128)S(1)}, f32[8,128]{1,0:T(8,128)}, u32[]{:S(2)}) copy-start(f32[8,128]{1,0:T(8,128)} %get-tuple-element.5) | copy-start | bytes 12292
